TPU v7x, 32 devices: a whole 2x2x4 slice. The times are simulated.
32 devices in a mesh: dp: 2 (over x), row: 4 (over y, core), col: 4 (over z).
Axes of the slice: x: 2, y: 2, z: 4, core: 2. Of those that a mesh axis runs over, the one named last changes fastest.
Arguments:
- tokens: bfloat16 [768, 39200], P('row', ('dp', 'col')), may hold values from -6 to 6
- grad_out: bfloat16 [768, 39200], P('row', ('dp', 'col')), may hold values from -6 to 6
- adapter_index: int32 [8, 1], replicated, may hold values from 0 to 7
- norm1_gain: bfloat16 [768], P('row'), may hold values from 0.099609375 to 1.8984375
- norm2_gain: bfloat16 [768], P('row'), may hold values from 0.099609375 to 1.8984375
- qkv_weight: bfloat16 [768, 2304], P('row', 'col'), may hold values from -0.21875 to 0.21875
- proj_weight: bfloat16 [768, 768], P('col', 'row'), may hold values from -0.875 to 0.875
- fc1_weight: bfloat16 [768, 3072], P('row', 'col'), may hold values from -0.21875 to 0.21875
- fc2_weight: bfloat16 [768, 3072], P('row', 'col'), may hold values from -0.109375 to 0.109375
- rel_h: bfloat16 [27, 64], replicated, may hold values from -0.59765625 to 0.59765625
- rel_w: bfloat16 [27, 64], replicated, may hold values from -0.59765625 to 0.59765625
- qkv_down: bfloat16 [8, 768, 16], P(None, 'row'), may hold values from -0.21875 to 0.21875
- qkv_up: bfloat16 [8, 16, 2304], P(None, None, 'col'), may hold values from -0.75 to 0.75
- proj_down: bfloat16 [8, 768, 16], P(None, 'col'), may hold values from -0.21875 to 0.21875
- proj_up: bfloat16 [8, 16, 768], P(None, None, 'row'), may hold values from -0.75 to 0.75
- fc1_down: bfloat16 [8, 768, 16], P(None, 'row'), may hold values from -0.21875 to 0.21875
- fc1_up: bfloat16 [8, 16, 3072], P(None, None, 'col'), may hold values from -0.75 to 0.75
- fc2_down: bfloat16 [8, 3072, 16], P(None, 'col'), may hold values from -0.109375 to 0.109375
- fc2_up: bfloat16 [8, 16, 768], P(None, None, 'row'), may hold values from -0.75 to 0.75
Outputs:
- out: bfloat16 [768, 39200], P('row', ('dp', 'col'))
- tokens_grad: float32 [768, 39200], P('row', ('dp', 'col'))
- qkv_down_grad: float32 [8, 768, 16], P(None, 'row')
- qkv_up_grad: float32 [8, 16, 2304], P(None, None, 'col')
- proj_down_grad: float32 [8, 768, 16], P(None, 'col')
- proj_up_grad: float32 [8, 16, 768], P(None, None, 'row')
- fc1_down_grad: float32 [8, 768, 16], P(None, 'row')
- fc1_up_grad: float32 [8, 16, 3072], P(None, None, 'col')
- fc2_down_grad: float32 [8, 3072, 16], P(None, 'col')
- fc2_up_grad: float32 [8, 16, 768], P(None, None, 'row')
Inputs may be any that keep to these rules, and one draw needn't show every extreme that they name: `adapter_index`: every one of the 8 adapters is chosen by at least one image.
All inputs are finite; a program needn't handle non-finite values.
Results may differ from a plain program's by a relative error of at most 0.015.
Values may be sent and summed in bfloat16 or wider, within the bound.
No kernel may reach another device: no remote copies, remote signals or barrier semaphores. Data moves between devices by JAX's collectives and lax.ppermute only.
A program may use at most 448 MiB of HBM per device.

v0:
```python
import functools

import jax
import jax.numpy as jnp
import numpy as np
from jax import lax
from jax.experimental import pallas as pl
from jax.experimental.pallas import tpu as pltpu
from jax.sharding import PartitionSpec as P

D = 768
HD = 64
WIN = 14
SLOTS = WIN * WIN
SIDE = 64
ADAPT = 8
NWIN = 5
IMG_TOK = NWIN * NWIN * SLOTS
RANK = 16
EDGE = SIDE - (NWIN - 1) * WIN
QUART = D // 4
FULLR = 208
KEYS = 208
EDGER = EDGE * WIN
CORNR = EDGE * EDGE
ROWS = 4 * FULLR + 2 * EDGER + CORNR
HALF = ROWS // 2
HBLK = QUART // 2
EPSILON = 1e-06
BF = jnp.bfloat16
F32 = jnp.float32
VMEM_LIMIT = 60 * 1024 * 1024

FULL, RIGHT, BOTTOM, CORNER = 0, 1, 2, 3
NQ = (FULLR, EDGER, EDGER, CORNR)
OFFS = (0, 4 * FULLR, 4 * FULLR + EDGER, 4 * FULLR + 2 * EDGER)


def slot_order(kind):
    rows = EDGE if kind in (BOTTOM, CORNER) else WIN
    cols = EDGE if kind in (RIGHT, CORNER) else WIN
    kept = [a * WIN + b for a in range(rows) for b in range(cols)]
    rest = [s for s in range(SLOTS) if s not in set(kept)]
    return kept, kept + rest


def build_tables():
    shift = np.zeros((4, FULLR, 128), np.int32)
    keys = np.zeros((4, KEYS, 128), np.float32)
    for kind in range(4):
        kept, order = slot_order(kind)
        for i, s in enumerate(kept):
            for base in (0, 64):
                shift[kind, i, base : base + 32] = WIN - 1 - s // WIN
                shift[kind, i, base + 32 : base + 64] = WIN - 1 - s % WIN
        spare = order[0] if kind == FULL else order[-1]
        for i, s in enumerate(order + [spare] * (KEYS - SLOTS)):
            for base in (0, 64):
                keys[kind, i, base + s // WIN] = 1.0
                keys[kind, i, base + 32 + s % WIN] = 1.0
    return shift, keys.astype(jnp.bfloat16)


SHIFT_NP, KEYS_NP = build_tables()


def nn(a, b):
    return jnp.dot(a, b, preferred_element_type=F32)


def nt(a, b):
    return lax.dot_general(a, b, (((1,), (1,)), ((), ())), preferred_element_type=F32)


def tn(a, b):
    return lax.dot_general(a, b, (((0,), (0,)), ((), ())), preferred_element_type=F32)


def vm():
    return pl.BlockSpec(memory_space=pltpu.VMEM)


def sm():
    return pl.BlockSpec(memory_space=pltpu.SMEM)


def params(**kw):
    return pltpu.CompilerParams(vmem_limit_bytes=VMEM_LIMIT, **kw)


def cost(us):
    return pl.CostEstimate(flops=int(us * 9e8), transcendentals=0, bytes_accessed=0)


def place_window(kind, count, shift, width, spare=-100000):
    row = lax.broadcasted_iota(jnp.int32, (count, width), 0)
    lane = lax.broadcasted_iota(jnp.int32, (count, width), 1)
    if kind in (RIGHT, CORNER):
        src = (row // EDGE) * WIN + row % EDGE
    else:
        src = jnp.where(row < SLOTS, row, spare)
    return (lane == src + shift).astype(F32).astype(BF)


def window_list(dest):
    items = [(FULL, FULLR * j, NWIN * dest + j) for j in range(4)]
    items.append((RIGHT, OFFS[1], NWIN * dest + 4))
    items.append((BOTTOM, OFFS[2], NWIN * 4 + dest))
    if dest == 3:
        items.append((CORNER, OFFS[3], NWIN * NWIN - 1))
    return items


def span_of(window):
    start = SLOTS * window
    low = start // 128 * 128
    high = min(-(-(start + SLOTS) // 128) * 128, IMG_TOK)
    return low, high, start - low


def pack_kernel(where_ref, x_ref, out_ref, rows_ref, *, spare):
    mine = where_ref[0]
    for dest in range(4):
        if dest != 3:
            rows_ref[OFFS[3] :, :] = jnp.zeros((CORNR, QUART), BF)
        for kind, offset, window in window_list(dest):
            low, high, moved = span_of(window)
            pick = place_window(kind, NQ[kind], moved, high - low, spare)
            rows_ref[offset : offset + NQ[kind], :] = nt(pick, x_ref[:, low:high]).astype(BF)
        slot = jnp.bitwise_xor(mine, dest)
        out_ref[slot, :, :QUART] = rows_ref[:HALF, :]
        out_ref[slot, :, QUART:] = rows_ref[HALF:, :]


def pack(where, x, spare=-100000):
    return pl.pallas_call(
        functools.partial(pack_kernel, spare=spare),
        out_shape=jax.ShapeDtypeStruct((4, HALF, 2 * QUART), BF),
        in_specs=[sm(), vm()],
        out_specs=vm(),
        scratch_shapes=[pltpu.VMEM((ROWS, QUART), BF)],
        compiler_params=params(),
        cost_estimate=cost(4),
        name="pack",
    )(where, x)


def unpack_kernel(where_ref, y0, y1, y2, y3, out_ref, acc_ref, rows_ref):
    mine = where_ref[0]
    acc_ref[...] = jnp.zeros_like(acc_ref)
    for slot, y in enumerate((y0, y1, y2, y3)):
        rows_ref[slot, :HALF, :] = y[:, :QUART]
        rows_ref[slot, HALF:, :] = y[:, QUART:]
    for source in range(4):
        slot = jnp.bitwise_xor(mine, source)
        for kind, offset, window in window_list(source):
            low, high, moved = span_of(window)
            pick = place_window(kind, NQ[kind], moved, high - low)
            acc_ref[:, low:high] += tn(rows_ref[slot, offset : offset + NQ[kind], :], pick)
    out_ref[...] = acc_ref[:, :IMG_TOK].astype(out_ref.dtype)


def unpack(where, pieces, dtype):
    return pl.pallas_call(
        unpack_kernel,
        out_shape=jax.ShapeDtypeStruct((QUART, IMG_TOK), dtype),
        in_specs=[sm()] + [vm()] * 4,
        out_specs=vm(),
        scratch_shapes=[
            pltpu.VMEM((QUART, -(-IMG_TOK // 128) * 128), F32),
            pltpu.VMEM((4, ROWS, QUART), BF),
        ],
        compiler_params=params(),
        cost_estimate=cost(4),
        name="unpack",
    )(where, *pieces)


def join_pieces(pieces, dst_ref):
    for slot, piece in enumerate(pieces):
        dst_ref[:HALF, QUART * slot : QUART * (slot + 1)] = piece[:, :QUART]
        dst_ref[HALF:, QUART * slot : QUART * (slot + 1)] = piece[:, QUART:]


def split_pieces(src_ref, out_ref):
    for slot in range(4):
        out_ref[slot, :, :QUART] = src_ref[:HALF, QUART * slot : QUART * (slot + 1)]
        out_ref[slot, :, QUART:] = src_ref[HALF:, QUART * slot : QUART * (slot + 1)]


def weight_pack_kernel(where_ref, qkv_w, proj_w, alpha_ref, beta_ref, alpha_half, beta_half):
    heads = qkv_w.shape[1] // (3 * HD)
    for h in range(heads):
        for t in range(3):
            ref, base = (alpha_ref, QUART * t) if t < 2 else (beta_ref, 0)
            ref[:, base + HD * h : base + HD * (h + 1)] = qkv_w[:, HD * (3 * h + t) : HD * (3 * h + t + 1)]
    beta_ref[:, QUART:] = proj_w[...]
    rows = pl.ds(pl.multiple_of(where_ref[1] * HBLK, 32), HBLK)
    alpha_half[...] = alpha_ref[rows, :]
    beta_half[...] = beta_ref[rows, :]


def weight_pack(where, qkv_w, proj_w):
    s = lambda *shape: jax.ShapeDtypeStruct(shape, BF)
    return pl.pallas_call(
        weight_pack_kernel,
        out_shape=(s(QUART, 2 * QUART), s(QUART, 2 * QUART), s(HBLK, 2 * QUART), s(HBLK, 2 * QUART)),
        in_specs=[sm(), vm(), vm()],
        out_specs=[vm()] * 4,
        compiler_params=params(),
        cost_estimate=cost(2),
        name="weight_pack",
    )(where, qkv_w, proj_w)


def adapter_pack_kernel(
    pick_ref, qkv_up, proj_dn, fc1_up, fc2_dn, qkv_dn, fc1_dn, proj_up, fc2_up, send_ref, row_ref,
):
    heads = qkv_up.shape[2] // (3 * HD)
    for j in range(4):
        a = pick_ref[j]
        for h in range(heads):
            for t in range(3):
                send_ref[j, :RANK, QUART * t + HD * h : QUART * t + HD * (h + 1)] = qkv_up[
                    a, :, HD * (3 * h + t) : HD * (3 * h + t + 1)
                ]
        send_ref[j, :RANK, 3 * QUART :] = proj_dn[a]
        send_ref[j, RANK : 2 * RANK, :] = fc1_up[a]
        send_ref[j, 2 * RANK :, :] = fc2_dn[a]
    for i, ref in enumerate((qkv_dn, fc1_dn, proj_up, fc2_up)):
        row_ref[:, QUART * i : QUART * (i + 1)] = ref[pick_ref[0]]


def adapter_pack(pick, *mats):
    s = lambda *shape: jax.ShapeDtypeStruct(shape, BF)
    return pl.pallas_call(
        adapter_pack_kernel,
        out_shape=(s(4, 3 * RANK, D), s(RANK, D)),
        in_specs=[sm()] + [vm()] * 8,
        out_specs=[vm()] * 2,
        compiler_params=params(),
        cost_estimate=cost(2),
        name="adapter_pack",
    )(pick, *mats)


def alpha_block(k, j):
    part = k
    if j == 0:
        return [(part, 0, QUART, None)]
    return [
        (part, QUART + HBLK * (j - 1), HBLK, 0),
        (part, QUART + 3 * HBLK + HBLK * (j - 1), HBLK, 1),
    ]


def beta_block(k, j):
    core, cross = k % 2, k // 2
    base = 3 * core
    if j == 0 and not cross:
        return [(base, 0, QUART, None)]
    row = 0 if j == 0 else HBLK + QUART * (j - 1) + HBLK * cross
    return [(base + 1, row, HBLK, 0), (base + 2, row, HBLK, 1)]


def block_dst(start, flag, half):
    if flag is None:
        return start
    offset = half if flag == 0 else 1 - half
    return pl.multiple_of(start + offset * HBLK, 32)


def prep1_kernel(
    where_ref, p0, p1, p2, p3, q0, q1, q2, q3, q4, q5, r0, r1, r2, r3, a0, a1, a2, a3,
    wqkv_ref, wproj_ref, dqkv, uqkv, dproj, uproj, d1, u1, d2, u2,
):
    half = where_ref[1]
    for j, a in enumerate((a0, a1, a2, a3)):
        for t in range(3):
            uqkv[:, D * t + QUART * j : D * t + QUART * (j + 1)] = a[:RANK, QUART * t : QUART * (t + 1)]
        dproj[:, QUART * j : QUART * (j + 1)] = a[:RANK, 3 * QUART :]
        u1[:, D * j : D * (j + 1)] = a[RANK : 2 * RANK, :]
        d2[:, D * j : D * (j + 1)] = a[2 * RANK :, :]
    for k, ref in enumerate((r0, r1, r2, r3)):
        for i, dst in enumerate((dqkv, d1, uproj, u2)):
            dst[:, QUART * k : QUART * (k + 1)] = ref[:, QUART * i : QUART * (i + 1)]
    alpha, beta = (p0, p1, p2, p3), (q0, q1, q2, q3, q4, q5)
    for k in range(4):
        for j in range(4):
            for part, row, count, flag in alpha_block(k, j):
                rows = pl.ds(block_dst(QUART * k, flag, half), count)
                for t in range(2):
                    wqkv_ref[rows, D * t + QUART * j : D * t + QUART * (j + 1)] = alpha[part][
                        row : row + count, QUART * t : QUART * (t + 1)
                    ]
            for part, row, count, flag in beta_block(k, j):
                rows = pl.ds(block_dst(QUART * k, flag, half), count)
                wqkv_ref[rows, 2 * D + QUART * j : 2 * D + QUART * (j + 1)] = beta[part][
                    row : row + count, :QUART
                ]
                rows = pl.ds(block_dst(QUART * j, flag, half), count)
                wproj_ref[rows, QUART * k : QUART * (k + 1)] = beta[part][row : row + count, QUART:]
    for k in range(4):
        rows = slice(QUART * k, QUART * (k + 1))
        for t in range(3):
            cols = slice(D * t, D * (t + 1))
            low = tn(dqkv[:, rows], uqkv[:, cols])
            wqkv_ref[rows, cols] = (wqkv_ref[rows, cols].astype(F32) + low).astype(BF)
        low = tn(dproj[:, rows], uproj[...])
        wproj_ref[rows, :] = (wproj_ref[rows, :].astype(F32) + low).astype(BF)


def prep1(where, alpha, beta, rows, cols):
    s = lambda *shape: jax.ShapeDtypeStruct(shape, BF)
    return pl.pallas_call(
        prep1_kernel,
        out_shape=(
            s(D, 3 * D), s(D, D), s(RANK, D), s(RANK, 3 * D), s(RANK, D), s(RANK, D),
            s(RANK, D), s(RANK, 4 * D), s(RANK, 4 * D), s(RANK, D),
        ),
        in_specs=[sm()] + [vm()] * 18,
        out_specs=[vm()] * 10,
        compiler_params=params(),
        cost_estimate=cost(7),
        name="attention_weights",
    )(where, *alpha, *beta, *rows, *cols)


def normalize(values):
    center = jnp.sum(values, axis=1, keepdims=True) / D
    shifted = values - center
    inv_std = lax.rsqrt(jnp.sum(shifted * shifted, axis=1, keepdims=True) / D + EPSILON)
    return shifted * inv_std, inv_std


def norm_back(grad, normed, inv_std):
    first = jnp.sum(grad, axis=1, keepdims=True) / D
    second = jnp.sum(grad * normed, axis=1, keepdims=True) / D
    return inv_std * (grad - first - normed * second)


def barrel(values, amount, left):
    for bit in (1, 2, 4, 8):
        moved = pltpu.roll(values, (128 - bit) if left else bit, 1)
        values = jnp.where((amount & bit) != 0, moved, values)
    return values


def low_half(count):
    return lax.broadcasted_iota(jnp.int32, (count, 128), 1) < HD


def pad_rows(tile):
    if tile.shape[0] == KEYS:
        return tile
    return jnp.concatenate([tile, jnp.zeros((KEYS - tile.shape[0], tile.shape[1]), tile.dtype)], axis=0)


def live_rows():
    return lax.broadcasted_iota(jnp.int32, (KEYS, 128), 0) < SLOTS


UNROLL = 6
UNROLL_BACK = 6


def pair_columns(pair):
    return tuple(pl.ds(pl.multiple_of(D * t + 128 * pair, 128), 128) for t in range(3))


def attend_window(kind, row0, qkv_ref, att_ref, exp_ref, inv_ref, rel_ref, shift_ref, keys_ref):
    count = NQ[kind]
    rows = pl.ds(row0, count)
    low_q, low_k = low_half(count), low_half(KEYS)
    live = live_rows()
    ones = jnp.where(live, 1.0, 0.0).astype(BF)
    amount = shift_ref[kind, :count, :]
    onehot = keys_ref[kind]

    def one_pair(pair, carry):
        cols, kcols, vcols = pair_columns(pair)
        q_tile = qkv_ref[rows, cols]
        k_tile = pad_rows(qkv_ref[rows, kcols] * BF(HD**-0.5))
        v_tile = pad_rows(qkv_ref[rows, vcols])
        if kind == FULL:
            v_tile = jnp.where(live, v_tile, 0).astype(BF)
        rel = barrel(nn(q_tile, rel_ref[...]), amount, True).astype(BF)
        both = []
        for odd in range(2):
            if odd:
                q_aug, k_aug = jnp.where(low_q, rel, q_tile), jnp.where(low_k, onehot, k_tile)
                v_aug = jnp.where(low_k, ones, v_tile)
            else:
                q_aug, k_aug = jnp.where(low_q, q_tile, rel), jnp.where(low_k, k_tile, onehot)
                v_aug = jnp.where(low_k, v_tile, ones)
            scores = nt(q_aug, k_aug)
            exponent = jnp.exp(scores - jnp.max(scores, axis=1, keepdims=True)).astype(BF)
            exp_ref[2 * pair + odd, rows, :] = exponent
            both.append(nn(exponent, v_aug))
        inverse = 1.0 / pltpu.roll(jnp.where(low_q, both[1], both[0]), HD, 1)
        inv_ref[rows, cols] = inverse
        att_ref[rows, cols] = (jnp.where(low_q, both[0], both[1]) * inverse).astype(BF)
        return carry

    lax.fori_loop(0, D // 128, one_pair, 0, unroll=UNROLL)


PARTS = ((FULL, FULL), (FULL, FULL), (RIGHT, BOTTOM, CORNER))
PART_ROWS = tuple(sum(NQ[kind] for kind in part) for part in PARTS)
PART_OFFS = (0, PART_ROWS[0], PART_ROWS[0] + PART_ROWS[1])


def qkv_kernel(x0, x1, x2, x3, gain_ref, wqkv_ref, x_ref, hid_ref, qkv_a, qkv_b, qkv_c):
    join_pieces((x0, x1, x2, x3), x_ref)
    gain = gain_ref[...]

    def norm_step(i, carry):
        rows = pl.ds(pl.multiple_of(i * 112, 16), 112)
        normed, _ = normalize(x_ref[rows, :].astype(F32))
        hid_ref[rows, :] = (normed * gain).astype(BF)
        return carry

    lax.fori_loop(0, ROWS // 112, norm_step, 0)
    for ref, offset, count in zip((qkv_a, qkv_b, qkv_c), PART_OFFS, PART_ROWS):
        hid = hid_ref[offset : offset + count, :]
        for t in range(3):
            cols = slice(D * t, D * (t + 1))
            ref[:, cols] = nn(hid, wqkv_ref[:, cols]).astype(BF)
    for w in range(4):
        hid_ref[FULLR * w + SLOTS : FULLR * (w + 1), :] = jnp.zeros((FULLR - SLOTS, D), BF)


def qkv_rows(pieces, gain, wqkv):
    s = lambda *shape: jax.ShapeDtypeStruct(shape, BF)
    return pl.pallas_call(
        qkv_kernel,
        out_shape=(s(ROWS, D), s(ROWS, D)) + tuple(s(n, 3 * D) for n in PART_ROWS),
        in_specs=[vm()] * 6,
        out_specs=[vm()] * 5,
        compiler_params=params(),
        cost_estimate=cost(12),
        name="norm_and_qkv",
    )(*pieces, gain, wqkv)


def attention_kernel(qkv_ref, rel_ref, shift_ref, keys_ref, att_ref, exp_ref, inv_ref, *, kinds):
    refs = (qkv_ref, att_ref, exp_ref, inv_ref, rel_ref, shift_ref, keys_ref)
    if kinds[0] == FULL:

        def step(w, carry):
            attend_window(FULL, pl.multiple_of(w * FULLR, 16), *refs)
            return carry

        lax.fori_loop(0, len(kinds), step, 0)
    else:
        row = 0
        for kind in kinds:
            attend_window(kind, row, *refs)
            row += NQ[kind]


def attention(part, qkv, rel, shift, keys):
    rows = PART_ROWS[part]
    s = lambda *shape, dtype=BF: jax.ShapeDtypeStruct(shape, dtype)
    return pl.pallas_call(
        functools.partial(attention_kernel, kinds=PARTS[part]),
        out_shape=(s(rows, D), s(D // HD, rows, KEYS), s(rows, D, dtype=F32)),
        in_specs=[vm()] * 4,
        out_specs=[vm()] * 3,
        compiler_params=params(),
        cost_estimate=cost(10),
        name="attention_forward",
    )(qkv, rel, shift, keys)


def project_kernel(x_ref, att_a, att_b, att_c, wproj_ref, middle_ref):
    for ref, offset, count in zip((att_a, att_b, att_c), PART_OFFS, PART_ROWS):
        rows = slice(offset, offset + count)
        middle_ref[rows, :] = x_ref[rows, :].astype(F32) + nn(ref[...], wproj_ref[...])


def project(x, atts, wproj):
    return pl.pallas_call(
        project_kernel,
        out_shape=jax.ShapeDtypeStruct((ROWS, D), F32),
        in_specs=[vm()] * 5,
        out_specs=vm(),
        compiler_params=params(),
        cost_estimate=cost(5),
        name="projection",
    )(x, *atts, wproj)


CHUNK = 512


def mlp_kernel(
    where_ref, middle_ref, g0, g1, g2, g3, gain_ref,
    p0, p1, p2, p3, q0, q1, q2, q3, q4, q5, d1, u1, d2, u2,
    out_ref, gmid_ref, down1, up1, down2, up2,
    gm_ref, out_rows, h2_ref, acc_mlp, acc_gh, gu1, ad2, w1_ref, w2_ref, sem,
):
    half = where_ref[1]
    copies = []

    def fetch(src, dst):
        copies.append(pltpu.make_async_copy(src, dst, sem.at[len(copies)]))
        copies[-1].start()

    alpha, beta = (p0, p1, p2, p3), (q0, q1, q2, q3, q4, q5)
    for k in range(4):
        for j in range(4):
            for part, row, count, flag in alpha_block(k, j):
                rows = pl.ds(block_dst(QUART * k, flag, half), count)
                fetch(alpha[part].at[row : row + count, :], w1_ref.at[rows, D * j : D * (j + 1)])
            for part, row, count, flag in beta_block(k, j):
                rows = pl.ds(block_dst(QUART * k, flag, half), count)
                fetch(beta[part].at[row : row + count, :], w2_ref.at[rows, D * j : D * (j + 1)])
    join_pieces((g0, g1, g2, g3), gm_ref)
    for copy in copies:
        copy.wait()
    for k in range(4):
        rows = slice(QUART * k, QUART * (k + 1))
        for j in range(4):
            cols = slice(D * j, D * (j + 1))
            low = tn(d1[:, rows], u1[:, cols])
            w1_ref[rows, cols] = (w1_ref[rows, cols].astype(F32) + low).astype(BF)
            low = tn(u2[:, rows], d2[:, cols])
            w2_ref[rows, cols] = (w2_ref[rows, cols].astype(F32) + low).astype(BF)
    gain = gain_ref[...]
    down1[...] = jnp.zeros_like(down1)
    up1[...] = jnp.zeros_like(up1)
    down2[...] = jnp.zeros_like(down2)
    up2[...] = jnp.zeros_like(up2)

    def tile_step(t, carry):
        rows = pl.ds(pl.multiple_of(t * HALF, 16), HALF)
        normed, _ = normalize(middle_ref[rows, :])
        h2 = (normed * gain).astype(BF)
        h2_ref[...] = h2
        gm = gm_ref[rows, :]
        ad1 = nt(d1[...], h2).astype(BF)
        gu2 = nt(u2[...], gm).astype(BF)
        acc_mlp[...] = jnp.zeros_like(acc_mlp)
        acc_gh[...] = jnp.zeros_like(acc_gh)
        gu1[...] = jnp.zeros_like(gu1)
        ad2[...] = jnp.zeros_like(ad2)

        def chunk_step(c, inner_carry):
            cols = pl.ds(pl.multiple_of(c * CHUNK, CHUNK), CHUNK)
            w1 = w1_ref[:, cols]
            w2 = w2_ref[:, cols]
            inner = nn(h2_ref[...], w1)
            gact = nn(gm_ref[rows, :], w2)
            half = 0.5 * (1.0 + lax.erf(inner * 2**-0.5))
            act = (inner * half).astype(BF)
            slope = half + inner * (jnp.exp(-0.5 * inner * inner) * (2 * np.pi) ** -0.5)
            ginner = (gact * slope).astype(BF)
            acc_mlp[...] += nt(act, w2)
            acc_gh[...] += nt(ginner, w1)
            up1[:, cols] += nn(ad1, ginner)
            gu1[...] += nt(u1[:, cols], ginner)
            ad2[...] += nt(d2[:, cols], act)
            down2[:, cols] += nn(gu2, act)
            return inner_carry

        lax.fori_loop(0, 4 * D // CHUNK, chunk_step, 0)
        down1[...] += nn(gu1[...].astype(BF), h2_ref[...])
        up2[...] += nn(ad2[...].astype(BF), gm_ref[rows, :])
        middle = middle_ref[rows, :]
        out_rows[rows, :] = (middle + acc_mlp[...]).astype(BF)
        normed, inv_std = normalize(middle)
        gmid_ref[rows, :] = gm_ref[rows, :].astype(F32) + norm_back(acc_gh[...] * gain, normed, inv_std)
        return carry

    lax.fori_loop(0, 2, tile_step, 0)
    split_pieces(out_rows, out_ref)


def mlp(where, middle, pieces, gain, alpha, beta, d1, u1, d2, u2):
    s = lambda *shape, dtype=F32: jax.ShapeDtypeStruct(shape, dtype)
    return pl.pallas_call(
        mlp_kernel,
        out_shape=(
            s(4, HALF, 2 * QUART, dtype=BF), s(ROWS, D),
            s(RANK, D), s(RANK, 4 * D), s(RANK, 4 * D), s(RANK, D),
        ),
        in_specs=[sm()] + [vm()] * 6 + [pl.BlockSpec(memory_space=pl.ANY)] * 10 + [vm()] * 4,
        out_specs=[vm()] * 6,
        scratch_shapes=[
            pltpu.VMEM((ROWS, D), BF), pltpu.VMEM((ROWS, D), BF), pltpu.VMEM((HALF, D), BF),
            pltpu.VMEM((HALF, D), F32), pltpu.VMEM((HALF, D), F32),
            pltpu.VMEM((RANK, HALF), F32), pltpu.VMEM((RANK, HALF), F32),
            pltpu.VMEM((D, 4 * D), BF), pltpu.VMEM((D, 4 * D), BF),
            pltpu.SemaphoreType.DMA((4 * 4 * 4,)),
        ],
        compiler_params=params(),
        cost_estimate=cost(48),
        name="mlp_forward_backward",
    )(where, middle, *pieces, gain, *alpha, *beta, d1, u1, d2, u2)


def attend_back_window(
    kind, row0, qkv_ref, att_ref, exp_ref, inv_ref, gatt_ref, gqkv_ref, rel_ref, shift_ref, keys_ref
):
    count = NQ[kind]
    rows = pl.ds(row0, count)
    low_q, low_k = low_half(count), low_half(KEYS)
    live = live_rows()
    lane_k = lax.broadcasted_iota(jnp.int32, (KEYS, 128), 1) % HD
    lane_q = lax.broadcasted_iota(jnp.int32, (count, 128), 1) % HD
    ones = jnp.where(live & (lane_k < 2), 1.0, 0.0).astype(BF)
    across = jnp.where(
        low_half(128) != (lax.broadcasted_iota(jnp.int32, (128, 128), 0) < HD), -1.0, 0.0
    ).astype(BF)
    amount = shift_ref[kind, :count, :]
    onehot = keys_ref[kind]

    def one_pair(pair, carry):
        cols, kcols, vcols = pair_columns(pair)
        q_tile = qkv_ref[rows, cols]
        k_tile = pad_rows(qkv_ref[rows, kcols] * BF(HD**-0.5))
        v_tile = pad_rows(qkv_ref[rows, vcols])
        if kind == FULL:
            v_tile = jnp.where(live, v_tile, 0).astype(BF)
        go_tile = (gatt_ref[rows, cols].astype(F32) * inv_ref[rows, cols]).astype(BF)
        delta = nn((go_tile.astype(F32) * att_ref[rows, cols].astype(F32)).astype(BF), across)
        high = delta.astype(BF)
        rest = (delta - high.astype(F32)).astype(BF)
        delta = jnp.where(lane_q == 0, high, jnp.where(lane_q == 1, rest, 0)).astype(BF)
        q_t = q_tile.T
        go_t = go_tile.T
        gq, gk, gv = [], [], []
        for odd in range(2):
            if odd:
                go_aug, v_aug = jnp.where(low_q, delta, go_tile), jnp.where(low_k, ones, v_tile)
                k_aug = jnp.where(low_k, onehot, k_tile)
            else:
                go_aug, v_aug = jnp.where(low_q, go_tile, delta), jnp.where(low_k, v_tile, ones)
                k_aug = jnp.where(low_k, k_tile, onehot)
            exponent = exp_ref[2 * pair + odd, rows, :]
            gs = (exponent.astype(F32) * nt(go_aug, v_aug)).astype(BF)
            side = slice(HD * odd, HD * (odd + 1))
            gv.append(nn(go_t[side, :], exponent))
            gk.append(nn(q_t[side, :], gs))
            gq.append(nn(gs, k_aug))
        sums = barrel(jnp.where(low_q, gq[1], gq[0]), amount, False).astype(BF)
        gqkv_ref[rows, cols] = (jnp.where(low_q, gq[0], gq[1]) + nt(sums, rel_ref[...])).astype(BF)
        gk_tile = (jnp.concatenate(gk, axis=0) * HD**-0.5).astype(BF).T
        gv_tile = jnp.concatenate(gv, axis=0).astype(BF).T
        gqkv_ref[rows, kcols] = gk_tile[:count, :]
        gqkv_ref[rows, vcols] = gv_tile[:count, :]
        return carry

    lax.fori_loop(0, D // 128, one_pair, 0, unroll=UNROLL_BACK)


def attention_back_kernel(
    gmid_ref, hid_ref, qkv_a, qkv_b, qkv_c, att_a, att_b, att_c, exp_a, exp_b, exp_c, inv_a, inv_b, inv_c,
    wproj_ref, rel_ref, shift_ref, keys_ref, dqkv, uqkv, dproj, uproj,
    gqkv_ref, down_q, up_q, down_p, up_p, gb_ref, gatt_ref, att_ref,
):
    gb_ref[...] = gmid_ref[...].astype(BF)
    gatt_ref[...] = nt(gb_ref[...], wproj_ref[...]).astype(BF)
    for ref, offset, count in zip((att_a, att_b, att_c), PART_OFFS, PART_ROWS):
        att_ref[offset : offset + count, :] = ref[...]
    up_p[...] = nn(nt(dproj[...], att_ref[...]).astype(BF), gb_ref[...])
    down_p[...] = nn(nt(uproj[...], gb_ref[...]).astype(BF), att_ref[...])
    tables = (rel_ref, shift_ref, keys_ref)
    for part, parts in enumerate(
        ((qkv_a, att_a, exp_a, inv_a), (qkv_b, att_b, exp_b, inv_b), (qkv_c, att_c, exp_c, inv_c))
    ):
        span = pl.ds(PART_OFFS[part], PART_ROWS[part])
        refs = parts + (gatt_ref.at[span, :], gqkv_ref.at[span, :]) + tables
        if PARTS[part][0] == FULL:

            def step(w, carry, refs=refs):
                attend_back_window(FULL, pl.multiple_of(w * FULLR, 16), *refs)
                return carry

            lax.fori_loop(0, len(PARTS[part]), step, 0)
        else:
            row = 0
            for kind in PARTS[part]:
                attend_back_window(kind, row, *refs)
                row += NQ[kind]
    up_q[...] = nn(nt(dqkv[...], hid_ref[...]).astype(BF), gqkv_ref[...])
    down_q[...] = nn(nt(uqkv[...], gqkv_ref[...]).astype(BF), hid_ref[...])


def attention_back(gmid, hid, qkvs, atts, exps, invs, wproj, rel, shift, keys, dqkv, uqkv, dproj, uproj):
    s = lambda *shape, dtype=F32: jax.ShapeDtypeStruct(shape, dtype)
    return pl.pallas_call(
        attention_back_kernel,
        out_shape=(s(ROWS, 3 * D, dtype=BF), s(RANK, D), s(RANK, 3 * D), s(RANK, D), s(RANK, D)),
        in_specs=[vm()] * 22,
        out_specs=[vm()] * 5,
        scratch_shapes=[pltpu.VMEM((ROWS, D), BF)] * 3,
        compiler_params=params(),
        cost_estimate=cost(45),
        name="attention_backward",
    )(gmid, hid, *qkvs, *atts, *exps, *invs, wproj, rel, shift, keys, dqkv, uqkv, dproj, uproj)


def token_grad_kernel(gmid_ref, x_ref, gqkv_ref, gain_ref, wqkv_ref, out_ref, gh_ref, out_rows):
    gh_ref[...] = nt(gqkv_ref[...], wqkv_ref[...])
    gain = gain_ref[...]

    def norm_step(i, carry):
        rows = pl.ds(pl.multiple_of(i * 112, 16), 112)
        normed, inv_std = normalize(x_ref[rows, :].astype(F32))
        back = norm_back(gh_ref[rows, :] * gain, normed, inv_std)
        out_rows[rows, :] = (gmid_ref[rows, :] + back).astype(BF)
        return carry

    lax.fori_loop(0, ROWS // 112, norm_step, 0)
    split_pieces(out_rows, out_ref)


def token_grad(gmid, x, gqkv, gain, wqkv):
    return pl.pallas_call(
        token_grad_kernel,
        out_shape=jax.ShapeDtypeStruct((4, HALF, 2 * QUART), BF),
        in_specs=[vm()] * 5,
        out_specs=vm(),
        scratch_shapes=[pltpu.VMEM((ROWS, D), F32), pltpu.VMEM((ROWS, D), BF)],
        compiler_params=params(),
        cost_estimate=cost(14),
        name="token_gradient",
    )(gmid, x, gqkv, gain, wqkv)


def grad_pack_kernel(where_ref, down_q, up_q, down_p, up_p, down1, up1, down2, up2, out_ref, buf_ref):
    mine = where_ref[0]
    for k in range(4):
        for i, ref in enumerate((down_q, down1, up_p, up2)):
            buf_ref[k, :RANK, QUART * i : QUART * (i + 1)] = ref[:, QUART * k : QUART * (k + 1)]
    for dest in range(4):
        k = jnp.bitwise_xor(mine, dest)
        ranks = slice(RANK // 4 * dest, RANK // 4 * (dest + 1))
        for j in range(4):
            base = RANK + 12 * j
            for t in range(3):
                buf_ref[k, base : base + 4, QUART * t : QUART * (t + 1)] = up_q[
                    ranks, D * t + QUART * j : D * t + QUART * (j + 1)
                ]
            buf_ref[k, base : base + 4, 3 * QUART :] = down_p[ranks, QUART * j : QUART * (j + 1)]
            buf_ref[k, base + 4 : base + 8, :] = up1[ranks, D * j : D * (j + 1)]
            buf_ref[k, base + 8 : base + 12, :] = down2[ranks, D * j : D * (j + 1)]
    out_ref[...] = buf_ref[...].astype(BF)


def grad_pack(where, *grads):
    return pl.pallas_call(
        grad_pack_kernel,
        out_shape=jax.ShapeDtypeStruct((4, 4 * RANK, D), BF),
        in_specs=[sm()] + [vm()] * 8,
        out_specs=vm(),
        scratch_shapes=[pltpu.VMEM((4, 4 * RANK, D), F32)],
        compiler_params=params(),
        cost_estimate=cost(2),
        name="adapter_grad_pack",
    )(where, *grads)


def grad_sum_kernel(g0, g1, g2, g3, out_ref, buf_ref):
    total = g0[...].astype(F32) + g1[...].astype(F32) + g2[...].astype(F32) + g3[...].astype(F32)
    buf_ref[...] = jnp.zeros_like(buf_ref)
    for j in range(4):
        buf_ref[:RANK, :] = total[:RANK, :]
        buf_ref[RANK : RANK + 12, :] = total[RANK + 12 * j : RANK + 12 * (j + 1), :]
        out_ref[j] = buf_ref[...].astype(BF)


def grad_sum(pieces):
    return pl.pallas_call(
        grad_sum_kernel,
        out_shape=jax.ShapeDtypeStruct((4, 2 * RANK, D), BF),
        in_specs=[vm()] * 4,
        out_specs=vm(),
        scratch_shapes=[pltpu.VMEM((2 * RANK, D), F32)],
        compiler_params=params(),
        cost_estimate=cost(2),
        name="adapter_grad_sum",
    )(*pieces)


def grad_adapters_kernel(index_ref, x_ref, qkv_dn, fc1_dn, proj_up, fc2_up, rest_ref, acc_ref):
    acc_ref[...] = jnp.zeros_like(acc_ref)

    def add(i, carry):
        acc_ref[index_ref[i]] += x_ref[i].astype(F32)
        return carry

    lax.fori_loop(0, x_ref.shape[0], add, 0)
    for i, ref in enumerate((qkv_dn, fc1_dn, proj_up, fc2_up)):
        ref[...] = acc_ref[:, :RANK, QUART * i : QUART * (i + 1)]
    rest_ref[...] = acc_ref[:, RANK:, :].astype(BF)


def grad_adapters(index, x):
    s = lambda n, dtype=F32: jax.ShapeDtypeStruct((ADAPT, RANK, n), dtype)
    return pl.pallas_call(
        grad_adapters_kernel,
        out_shape=(s(QUART), s(QUART), s(QUART), s(QUART), s(D, BF)),
        in_specs=[sm(), vm()],
        out_specs=[vm()] * 5,
        scratch_shapes=[pltpu.VMEM((ADAPT, 2 * RANK, D), F32)],
        compiler_params=params(),
        cost_estimate=cost(2),
        name="adapter_grad_by_adapter",
    )(index, x)


def grad_join_kernel(where_ref, r0, r1, r2, r3, qkv_up, proj_dn, fc1_up, fc2_dn, buf_ref):
    mine = where_ref[0]
    heads = qkv_up.shape[2] // (3 * HD)
    for k, ref in enumerate((r0, r1, r2, r3)):
        buf_ref[jnp.bitwise_xor(mine, k)] = ref[...].astype(F32)
    for source in range(4):
        ranks = slice(RANK // 4 * source, RANK // 4 * (source + 1))
        for h in range(heads):
            for t in range(3):
                qkv_up[:, ranks, HD * (3 * h + t) : HD * (3 * h + t + 1)] = buf_ref[
                    source, :, 0:4, QUART * t + HD * h : QUART * t + HD * (h + 1)
                ]
        proj_dn[:, ranks, :] = buf_ref[source, :, 0:4, 3 * QUART :]
        fc1_up[:, ranks, :] = buf_ref[source, :, 4:8, :]
        fc2_dn[:, ranks, :] = buf_ref[source, :, 8:12, :]


def grad_join(where, pieces):
    s = lambda n: jax.ShapeDtypeStruct((ADAPT, RANK, n), F32)
    return pl.pallas_call(
        grad_join_kernel,
        out_shape=(s(3 * QUART), s(QUART), s(D), s(D)),
        in_specs=[sm()] + [vm()] * 4,
        out_specs=[vm()] * 4,
        scratch_shapes=[pltpu.VMEM((4, ADAPT, RANK, D), F32)],
        compiler_params=params(),
        cost_estimate=cost(2),
        name="adapter_grad_join",
    )(where, *pieces)


def flip(values, axis, distance):
    size = lax.axis_size(axis)
    return lax.ppermute(values, axis, [(i, i ^ distance) for i in range(size)])


def exchange(slots, axis):
    return [slots[0]] + [flip(slots[k], axis, k) for k in range(1, 4)]


def after(values, *deps):
    return lax.optimization_barrier((tuple(values), deps))[0]


def col_halves(half):
    return jnp.concatenate([flip(half, "col", j) for j in range(1, 4)], axis=0)


def col_pairs(half, other_row):
    two = jnp.concatenate([half, other_row], axis=0)
    return jnp.concatenate([other_row] + [flip(two, "col", j) for j in range(1, 4)], axis=0)


def rel_matrix(rel_h, rel_w):
    pad = jnp.zeros((32 - (2 * WIN - 1), HD), BF)
    block = jnp.concatenate([rel_h[::-1], pad, rel_w[::-1], pad], axis=0).T
    zero = jnp.zeros((HD, HD), BF)
    return jnp.concatenate(
        [jnp.concatenate([zero, block], axis=1), jnp.concatenate([block, zero], axis=1)], axis=0
    )


def body(
    tokens, grad_out, adapter_index, norm1_gain, norm2_gain, qkv_weight, proj_weight, fc1_weight, fc2_weight,
    rel_h, rel_w, qkv_down, qkv_up, proj_down, proj_up, fc1_down, fc1_up, fc2_down, fc2_up,
):
    members = lax.axis_size("col")
    batches = lax.axis_size("dp")
    row_index, col_index, dp_index = lax.axis_index("row"), lax.axis_index("col"), lax.axis_index("dp")
    half = dp_index % 2
    where = jnp.stack([row_index, half]).astype(jnp.int32)
    slot_images = (
        jnp.bitwise_xor(dp_index, jnp.arange(batches, dtype=jnp.int32))[:, None] * members
        + jnp.bitwise_xor(col_index, jnp.arange(members, dtype=jnp.int32))[None, :]
    ).reshape(-1)
    slot_adapters = jnp.sum(
        jnp.where(
            slot_images[:, None] == jnp.arange(adapter_index.shape[0], dtype=jnp.int32)[None, :],
            adapter_index[:, 0][None, :],
            0,
        ),
        axis=1,
    )
    pick = jnp.concatenate([slot_adapters[:4], half[None]]).astype(jnp.int32)
    swap = lambda m: jnp.swapaxes(m, 1, 2)

    rel = rel_matrix(rel_h, rel_w)
    shift, keys = jnp.asarray(SHIFT_NP), jnp.asarray(KEYS_NP)

    alpha_own, beta_own, alpha_half, beta_half = weight_pack(where, qkv_weight, proj_weight)
    b0 = flip(beta_half, "row", 2)
    alpha_near = col_halves(alpha_half)
    token_slots = pack(where, tokens, 0)
    x_pieces = exchange(token_slots, "row")
    beta_near = col_pairs(beta_half, b0)
    alpha_far = flip(alpha_near, "dp", 1)
    g = jnp.concatenate([alpha_own, alpha_near, alpha_far], axis=0)
    g, _ = after((g, x_pieces[1]), x_pieces[2])
    gy = flip(g, "row", 2)
    beta_far = flip(beta_near, "dp", 1)
    beta1 = [beta_own, beta_near, beta_far] + [flip(m, "row", 1) for m in (beta_own, beta_near, beta_far)]

    gains = jnp.stack([norm1_gain, norm2_gain]).astype(F32)
    send, row_adapters = adapter_pack(
        pick, qkv_up, swap(proj_down), fc1_up, swap(fc2_down), swap(qkv_down), swap(fc1_down), proj_up, fc2_up,
    )
    gains, send, row_adapters = after((gains, send, row_adapters), beta_near)
    col_adapters = exchange(send, "col")
    gain_all = jnp.concatenate(exchange([gains] * 4, "row"), axis=1)
    gain1, gain2 = gain_all[0:1], gain_all[1:2]
    row_adapters = exchange([row_adapters] * 4, "row")

    fc1_half = lax.dynamic_slice_in_dim(fc1_weight, half * HBLK, HBLK, 0)
    fc2_half = lax.dynamic_slice_in_dim(fc2_weight, half * HBLK, HBLK, 0)
    c0 = flip(fc2_half, "row", 2)
    fc1_half, fc2_half, c0 = after((fc1_half, fc2_half, c0), col_adapters[1], col_adapters[2], col_adapters[3])
    fc1_near = col_halves(fc1_half)
    fc2_near = col_pairs(fc2_half, c0)
    fc1_far = flip(fc1_near, "dp", 1)
    h = jnp.concatenate([fc1_weight, fc1_near, fc1_far], axis=0)

    grad_slots = pack(where, grad_out)
    alpha1 = [g, flip(g, "row", 1), gy, flip(gy, "row", 1)]
    wqkv, wproj, dqkv, uqkv, dproj, uproj, d1, u1, d2, u2 = prep1(where, alpha1, beta1, row_adapters, col_adapters)
    x, hid, *qkvs = qkv_rows(x_pieces, gain1, wqkv)
    qkv0, h = after((qkvs[0], h), gy)
    hy = flip(h, "row", 2)
    part0 = attention(0, qkv0, rel, shift, keys)
    qkv1, fc2_near = after((qkvs[1], fc2_near), part0[0])
    fc2_far = flip(fc2_near, "dp", 1)
    part1 = attention(1, qkv1, rel, shift, keys)
    qkv2, hy, grad_slots = after((qkvs[2], hy, grad_slots), part1[0])
    g_pieces = exchange(grad_slots, "row")
    alpha2 = [h, flip(h, "row", 1), hy, flip(hy, "row", 1)]
    part2 = attention(2, qkv2, rel, shift, keys)
    atts, exps, invs = zip(part0, part1, part2)
    middle = project(x, atts, wproj)
    beta2 = [fc2_weight, fc2_near, fc2_far] + [flip(m, "row", 1) for m in (fc2_weight, fc2_near, fc2_far)]

    out_slots, gmid, down1, up1, down2, up2 = mlp(where, middle, g_pieces, gain2, alpha2, beta2, d1, u1, d2, u2)
    out_pieces = exchange(out_slots, "row")
    gqkv, down_q, up_q, down_p, up_p = attention_back(
        gmid, hid, qkvs, atts, exps, invs, wproj, rel, shift, keys, dqkv, uqkv, dproj, uproj
    )
    gqkv, down_q, up_q, down_p, up_p = after((gqkv, down_q, up_q, down_p, up_p), *out_pieces)
    packed = grad_pack(where, down_q, up_q, down_p, up_p, down1, up1, down2, up2)
    row_sums = exchange(packed, "row")
    back_slots = token_grad(gmid, x, gqkv, gain1, wqkv)
    back_slots, *row_sums = after((back_slots, *row_sums))
    back_pieces = exchange(back_slots, "row")
    summed = grad_sum(row_sums)
    images = jnp.stack(exchange(summed, "col"))
    step = 1
    while step < batches:
        images = jnp.concatenate([images, flip(images, "dp", step)], axis=0)
        step *= 2
    qkv_dn, fc1_dn, proj_upg, fc2_upg, rest = grad_adapters(slot_adapters.astype(jnp.int32), images)
    rests = [rest] + [flip(rest, "row", k) for k in range(1, 4)]
    qkv_upg, proj_dn, fc1_upg, fc2_dn = grad_join(where, rests)
    result = unpack(where, out_pieces, BF)
    grad_tokens = unpack(where, back_pieces, F32)
    return (
        result, grad_tokens,
        swap(qkv_dn), qkv_upg, swap(proj_dn), proj_upg, swap(fc1_dn), fc1_upg, swap(fc2_dn), fc2_upg,
    )


def solution(mesh):
    return jax.shard_map(
        body,
        mesh=mesh,
        in_specs=(
            P("row", ("dp", "col")), P("row", ("dp", "col")), P(), P("row"), P("row"),
            P("row", "col"), P("col", "row"), P("row", "col"), P("row", "col"), P(), P(),
            P(None, "row", None), P(None, None, "col"), P(None, "col", None), P(None, None, "row"),
            P(None, "row", None), P(None, None, "col"), P(None, "col", None), P(None, None, "row"),
        ),
        out_specs=(
            P("row", ("dp", "col")), P("row", ("dp", "col")),
            P(None, "row", None), P(None, None, "col"), P(None, "col", None), P(None, None, "row"),
            P(None, "row", None), P(None, None, "col"), P(None, "col", None), P(None, None, "row"),
        ),
        check_vma=False,
    )
```

profile of v0, /device:TPU:1, one launch (start us, length us, event | category | flops | bytes accessed | tf_op | source)
XLA Modules:
  0.0 372.3 jit_solution(6805089194483311973)
XLA Ops:
  3.2 4.2 %collective-permute-start.12 = (bf16[96,384]{1,0:T(8,128)(2,1)}, bf16[96,384]{1,0:T(8,128)(2,1)S(1)}, u32[]{:S(2)}, u32[]{:S(2)}) collective-permute-start(bf16[96,384]{1,0:T(8,128)(2,1)} %get-tuple-element.89), channel_id=1, source_target_pairs={{0,3},{1,2},{2,1},{3,0},{4,7},{5,6},{6,5},{7,4},{8,11},{9,10},{10,... | collective-permute-start | bytes 221192 | tf_op jit(solution)/shard_map/ppermute | solution.py:848
  14.9 4.3 %pack.2 = bf16[4,560,384]{2,1,0:T(8,128)(2,1)} custom-call(s32[2]{0:T(128)} %pad_add_fusion.where_ref, bf16[192,4900]{1,0:T(8,128)(2,1)} %x_ref.2), custom_call_target="tpu_custom_call" | custom-call | flops 3600000000 | tf_op jit(solution)/shard_map/pack/pallas_call | solution.py:136
  31.1 4.6 %collective-permute-done.4 = bf16[192,384]{1,0:T(8,128)(2,1)S(1)} collective-permute-done((bf16[192,384]{1,0:T(8,128)(2,1)S(1)}, bf16[192,384]{1,0:T(8,128)(2,1)S(1)}, u32[]{:S(2)}, u32[]{:S(2)}) %collective-permute-start.4) | collective-permute-done | bytes 147488 | tf_op jit(solution)/shard_map/ppermute | solution.py:848
  54.2 3.7 collective-permute-start.24
  68.4 8.5 %collective-permute-done.29 = bf16[96,768]{1,0:T(8,128)(2,1)S(1)} collective-permute-done((bf16[96,768]{1,0:T(8,128)(2,1)S(1)}, bf16[96,768]{1,0:T(8,128)(2,1)S(1)}, u32[]{:S(2)}, u32[]{:S(2)}) %collective-permute-start.29) | collective-permute-done | bytes 147488 | tf_op jit(solution)/shard_map/ppermute | solution.py:848
  76.9 10.1 %collective-permute-start.32 = (bf16[192,768]{1,0:T(8,128)(2,1)S(1)}, bf16[192,768]{1,0:T(8,128)(2,1)S(1)}, u32[]{:S(2)}, u32[]{:S(2)}) collective-permute-start(bf16[192,768]{1,0:T(8,128)(2,1)S(1)} %constant_dynamic-update-slice_fusion.16), channel_id=1, source_target_pairs={{0,1},{1,0},{2,3},{3,2},{4,5},{5,4},{6,7},{7,6},{8,9},{9,8},{10,11... | collective-permute-start | bytes 884744 | tf_op jit(solution)/shard_map/ppermute | solution.py:848
  87.7 3.5 collective-permute-start.19
  91.2 8.5 %collective-permute-done.33 = bf16[192,768]{1,0:T(8,128)(2,1)S(1)} collective-permute-done((bf16[192,768]{1,0:T(8,128)(2,1)S(1)}, bf16[192,768]{1,0:T(8,128)(2,1)S(1)}, u32[]{:S(2)}, u32[]{:S(2)}) %collective-permute-start.33) | collective-permute-done | bytes 294944 | tf_op jit(solution)/shard_map/ppermute | solution.py:848
  106.0 9.1 %collective-permute-done.31 = bf16[288,768]{1,0:T(8,128)(2,1)S(1)} collective-permute-done((bf16[288,768]{1,0:T(8,128)(2,1)S(1)}, bf16[288,768]{1,0:T(8,128)(2,1)S(1)}, u32[]{:S(2)}, u32[]{:S(2)}) %collective-permute-start.31) | collective-permute-done | bytes 442400 | tf_op jit(solution)/shard_map/ppermute | solution.py:848
  120.2 7.3 %attention_weights.1 = (bf16[768,2304]{1,0:T(8,128)(2,1)}, bf16[768,768]{1,0:T(8,128)(2,1)}, bf16[16,768]{1,0:T(8,128)(2,1)}, bf16[16,2304]{1,0:T(8,128)(2,1)}, ...) custom-call(s32[2]{0:T(128)} %pad_add_fusion.where_ref, ...), custom_call_target="tpu_custom_call" | custom-call | flops 6300000256 | tf_op jit(solution)/shard_map/attention_weights/pallas_call | solution.py:315
  129.5 10.6 %norm_and_qkv.1 = (bf16[1120,768]{1,0:T(8,128)(2,1)}, bf16[1120,768]{1,0:T(8,128)(2,1)}, bf16[416,2304]{1,0:T(8,128)(2,1)}, bf16[416,2304]{1,0:T(8,128)(2,1)}, bf16[288,2304]{1,0:T(8,128)(2,1)}) custom-call(bf16[560,384]{1,0:T(8,128)(2,1)} %get-tuple-element.173.x0, bf16[560,384]{1,0:T(8,128)(2,1)} %copy-done.17, bf16[560,384]{1,0:T(8,128)(2,1)} %copy-done.16, ...), custom_call_target="tpu_custom_call" | custom-call | flops 10800000000 | tf_op jit(solution)/shard_map/norm_and_qkv/pallas_call | solution.py:435
  141.6 11.1 %attention_forward.3 = (bf16[416,768]{1,0:T(8,128)(2,1)}, bf16[12,416,208]{2,1,0:T(8,128)(2,1)}, f32[416,768]{1,0:T(8,128)}) custom-call(bf16[416,2304]{1,0:T(8,128)(2,1)} %get-tuple-element.98.qkv_ref.qkv_a, bf16[128,128]{1,0:T(8,128)(2,1)} %fusion.2.rel_ref, s32[4,208,128]{2,1,0:T(8,128)} %constant.40.clone.shift_ref, ...), custom_call_target="tpu_custom_call" | custom-call | flops 8999999488 | tf_op jit(solution)/shard_map/attention_forward/pallas_call | solution.py:465
  153.0 4.3 %pack.3 = bf16[4,560,384]{2,1,0:T(8,128)(2,1)} custom-call(s32[2]{0:T(128)} %pad_add_fusion.where_ref, bf16[192,4900]{1,0:T(8,128)(2,1)} %x_ref.3), custom_call_target="tpu_custom_call" | custom-call | flops 3600000000 | tf_op jit(solution)/shard_map/pack/pallas_call | solution.py:136
  158.1 11.1 %attention_forward.4 = (bf16[416,768]{1,0:T(8,128)(2,1)}, bf16[12,416,208]{2,1,0:T(8,128)(2,1)}, f32[416,768]{1,0:T(8,128)}) custom-call(bf16[416,2304]{1,0:T(8,128)(2,1)} %get-tuple-element.103.qkv_ref.qkv_b, bf16[128,128]{1,0:T(8,128)(2,1)} %fusion.2.rel_ref, s32[4,208,128]{2,1,0:T(8,128)} %constant.40.clone.shift_ref, ...), custom_call_target="tpu_custom_call" | custom-call | flops 8999999488 | tf_op jit(solution)/shard_map/attention_forward/pallas_call | solution.py:465
  169.3 7.4 %collective-permute-done.41.q2 = bf16[672,768]{1,0:T(8,128)(2,1)} collective-permute-done((bf16[672,768]{1,0:T(8,128)(2,1)S(1)}, bf16[672,768]{1,0:T(8,128)(2,1)}, u32[]{:S(2)}, u32[]{:S(2)}) %collective-permute-start.41) | collective-permute-done | bytes 1032224 | tf_op jit(solution)/shard_map/ppermute | solution.py:848
  181.1 19.7 %attention_forward.5 = (bf16[288,768]{1,0:T(8,128)(2,1)}, bf16[12,288,208]{2,1,0:T(8,128)(2,1)}, f32[288,768]{1,0:T(8,128)}) custom-call(bf16[288,2304]{1,0:T(8,128)(2,1)} %get-tuple-element.107.qkv_ref.qkv_c, bf16[128,128]{1,0:T(8,128)(2,1)} %fusion.2.rel_ref, s32[4,208,128]{2,1,0:T(8,128)} %constant.40.clone.shift_ref, ...), custom_call_target="tpu_custom_call" | custom-call | flops 8999999488 | tf_op jit(solution)/shard_map/attention_forward/pallas_call | solution.py:465
  200.8 5.6 %projection.1.middle_ref = f32[1120,768]{1,0:T(8,128)} custom-call(bf16[1120,768]{1,0:T(8,128)(2,1)} %get-tuple-element.95.x_ref, bf16[416,768]{1,0:T(8,128)(2,1)} %get-tuple-element.99.att_a, bf16[416,768]{1,0:T(8,128)(2,1)} %get-tuple-element.104.att_b, bf16[288,768]{1,0:T(8,128)(2,1)} %get-tuple-element.108.att_c, ...), custom_call_target="tpu_custom_call" | custom-call | flops 4499999744 | tf_op jit(solution)/shard_map/projection/pallas_call | solution.py:483
  207.4 45.9 %mlp_forward_backward.1 = (bf16[4,560,384]{2,1,0:T(8,128)(2,1)}, f32[1120,768]{1,0:T(8,128)}, f32[16,768]{1,0:T(8,128)}, f32[16,3072]{1,0:T(8,128)}, f32[16,3072]{1,0:T(8,128)}, /*index=5*/f32[16,768]{1,0:T(8,128)}) custom-call(s32[2]{0:T(128)} %pad_add_fusion.where_ref, f32[1120,768]{1,0:T(8,128)} %projection.1.middle_ref, ...), custom_call_target="tpu_custom_call" | custom-call | flops 43200000000 | tf_op jit(solution)/shard_map/mlp_forward_backward/pallas_call | solution.py:582
  257.8 47.2 %attention_backward.1 = (bf16[1120,2304]{1,0:T(8,128)(2,1)}, f32[16,768]{1,0:T(8,128)}, f32[16,2304]{1,0:T(8,128)}, f32[16,768]{1,0:T(8,128)}, f32[16,768]{1,0:T(8,128)}) custom-call(f32[1120,768]{1,0:T(8,128)} %get-tuple-element.118.gmid_ref, bf16[1120,768]{1,0:T(8,128)(2,1)} %get-tuple-element.119.hid_ref, ...), custom_call_target="tpu_custom_call" | custom-call | flops 40499998720 | tf_op jit(solution)/shard_map/attention_backward/pallas_call | solution.py:693
  305.1 14.6 %token_gradient.1 = bf16[4,560,384]{2,1,0:T(8,128)(2,1)} custom-call(f32[1120,768]{1,0:T(8,128)} %get-tuple-element.118.gmid_ref, bf16[1120,768]{1,0:T(8,128)(2,1)} %get-tuple-element.95.x_ref, bf16[1120,2304]{1,0:T(8,128)(2,1)} %get-tuple-element.135.gqkv_ref, f32[1,768]{1,0:T(1,128)} %get-tuple-element.190.gain_ref, ...), custom_call_target="tpu_custom_call" | custom-call | flops 12600000512 | tf_op jit(solution)/shard_map/token_gradient/pallas_call | solution.py:721
  325.8 4.2 %unpack.2 = bf16[192,4900]{1,0:T(8,128)(2,1)} custom-call(s32[2]{0:T(128)} %pad_add_fusion.where_ref, bf16[560,384]{1,0:T(8,128)(2,1)} %get-tuple-element.165.y0, bf16[560,384]{1,0:T(8,128)(2,1)} %copy-done.20, bf16[560,384]{1,0:T(8,128)(2,1)} %copy-done.19, bf16[560,384]{1,0:T(8,128)(2,1)} %copy-done.18), custom_call_target="tpu_custom_call" | custom-call | flops 3600000000 | tf_op jit(solution)/shard_map/unpack/pallas_call | solution.py:164
  341.5 5.7 %collective-permute-done.57 = bf16[4,32,768]{2,1,0:T(8,128)(2,1)S(1)} collective-permute-done((bf16[4,32,768]{2,1,0:T(8,128)(2,1)S(1)}, bf16[4,32,768]{2,1,0:T(8,128)(2,1)S(1)}, u32[]{:S(2)}, u32[]{:S(2)}) %collective-permute-start.57) | collective-permute-done | bytes 196640 | tf_op jit(solution)/shard_map/ppermute | solution.py:848
  352.7 7.7 %collective-permute-done.52.y2 = bf16[560,384]{1,0:T(8,128)(2,1)S(1)} collective-permute-done((bf16[560,384]{1,0:T(8,128)(2,1)S(1)}, bf16[560,384]{1,0:T(8,128)(2,1)S(1)}, u32[]{:S(2)}, u32[]{:S(2)}) %collective-permute-start.52) | collective-permute-done | bytes 430112 | tf_op jit(solution)/shard_map/ppermute | solution.py:848
  361.4 4.9 %unpack.3 = f32[192,4900]{1,0:T(8,128)} custom-call(s32[2]{0:T(128)} %pad_add_fusion.where_ref, bf16[560,384]{1,0:T(8,128)(2,1)} %get-tuple-element.161.y0, bf16[560,384]{1,0:T(8,128)(2,1)} %copy-done.23, bf16[560,384]{1,0:T(8,128)(2,1)} %copy-done.22, bf16[560,384]{1,0:T(8,128)(2,1)} %copy-done.21), custom_call_target="tpu_custom_call" | custom-call | flops 3600000000 | tf_op jit(solution)/shard_map/unpack/pallas_call | solution.py:164
  (264 shorter events, 106.8 us)
Async XLA Ops:
  3.2 24.1 %collective-permute-start.12 = (bf16[96,384]{1,0:T(8,128)(2,1)}, bf16[96,384]{1,0:T(8,128)(2,1)S(1)}, u32[]{:S(2)}, u32[]{:S(2)}) collective-permute-start(bf16[96,384]{1,0:T(8,128)(2,1)} %get-tuple-element.89), channel_id=1, source_target_pairs={{0,3},{1,2},{2,1},{3,0},{4,7},{5,6},{6,5},{7,4},{8,11},{9,10},{10,... | collective-permute-start | bytes 221192 | tf_op jit(solution)/shard_map/ppermute | solution.py:848
  7.4 21.9 %collective-permute-start.11 = (bf16[96,384]{1,0:T(8,128)(2,1)}, bf16[96,384]{1,0:T(8,128)(2,1)S(1)}, u32[]{:S(2)}, u32[]{:S(2)}) collective-permute-start(bf16[96,384]{1,0:T(8,128)(2,1)} %get-tuple-element.89), channel_id=1, source_target_pairs={{0,2},{1,3},{2,0},{3,1},{4,6},{5,7},{6,4},{7,5},{8,10},{9,11},{10,... | collective-permute-start | bytes 221192 | tf_op jit(solution)/shard_map/ppermute | solution.py:848
  8.6 37.1 %collective-permute-start.27 = (bf16[96,768]{1,0:T(8,128)(2,1)S(1)}, bf16[96,768]{1,0:T(8,128)(2,1)S(1)}, u32[]{:S(2)}, u32[]{:S(2)}) collective-permute-start(bf16[96,768]{1,0:T(8,128)(2,1)S(1)} %constant_dynamic-slice_fusion), channel_id=1, source_target_pairs={{0,8},{4,12},{8,0},{12,4},{1,9},{5,13},{9,1},{13,5},{2,10},{6,14},... | collective-permute-start | bytes 442376 | tf_op jit(solution)/shard_map/ppermute | solution.py:848
  23.6 24.8 %collective-permute-start.1 = (bf16[560,384]{1,0:T(8,128)(2,1)S(1)}, bf16[560,384]{1,0:T(8,128)(2,1)S(1)}, u32[]{:S(2)}, u32[]{:S(2)}) collective-permute-start(bf16[560,384]{1,0:T(8,128)(2,1)S(1)} %get-tuple-element.171), channel_id=1, source_target_pairs={{0,8},{4,12},{8,0},{12,4},{1,9},{5,13},{9,1},{13,5},{2,10},{6,14},... | collective-permute-start | bytes 1290248 | tf_op jit(solution)/shard_map/ppermute | solution.py:848
  25.0 24.2 %collective-permute-start = (bf16[560,384]{1,0:T(8,128)(2,1)S(1)}, bf16[560,384]{1,0:T(8,128)(2,1)S(1)}, u32[]{:S(2)}, u32[]{:S(2)}) collective-permute-start(bf16[560,384]{1,0:T(8,128)(2,1)S(1)} %get-tuple-element.172), channel_id=1, source_target_pairs={{0,4},{4,0},{8,12},{12,8},{1,5},{5,1},{9,13},{13,9},{2,6},{6,2},{1... | collective-permute-start | bytes 1290248 | tf_op jit(solution)/shard_map/ppermute | solution.py:848
  59.2 44.5 %collective-permute-start.15 = (bf16[768,384]{1,0:T(8,128)(2,1)S(1)}, bf16[768,384]{1,0:T(8,128)(2,1)S(1)}, u32[]{:S(2)}, u32[]{:S(2)}) collective-permute-start(bf16[768,384]{1,0:T(8,128)(2,1)S(1)} %constant_dynamic-update-slice_fusion.6.p0), channel_id=1, source_target_pairs={{0,8},{4,12},{8,0},{12,4},{1,9},{5,13},{9,1},{13,5},{2,10},{6,14},... | collective-permute-start | bytes 1769480 | tf_op jit(solution)/shard_map/ppermute | solution.py:848
  60.7 42.6 %collective-permute-start.17 = (bf16[672,384]{1,0:T(8,128)(2,1)S(1)}, bf16[672,384]{1,0:T(8,128)(2,1)S(1)}, u32[]{:S(2)}, u32[]{:S(2)}) collective-permute-start(bf16[672,384]{1,0:T(8,128)(2,1)S(1)} %constant_dynamic-update-slice_fusion.2.q1), channel_id=1, source_target_pairs={{0,16},{16,0},{1,17},{17,1},{2,18},{18,2},{3,19},{19,3},{4,20},{20... | collective-permute-start | bytes 1548296 | tf_op jit(solution)/shard_map/ppermute | solution.py:848
  76.9 22.8 %collective-permute-start.33 = (bf16[192,768]{1,0:T(8,128)(2,1)S(1)}, bf16[192,768]{1,0:T(8,128)(2,1)S(1)}, u32[]{:S(2)}, u32[]{:S(2)}) collective-permute-start(bf16[192,768]{1,0:T(8,128)(2,1)S(1)} %constant_dynamic-update-slice_fusion.16), channel_id=1, source_target_pairs={{0,2},{1,3},{2,0},{3,1},{4,6},{5,7},{6,4},{7,5},{8,10},{9,11},{10,... | collective-permute-start | bytes 884744 | tf_op jit(solution)/shard_map/ppermute | solution.py:848
  76.9 26.4 %collective-permute-start.32 = (bf16[192,768]{1,0:T(8,128)(2,1)S(1)}, bf16[192,768]{1,0:T(8,128)(2,1)S(1)}, u32[]{:S(2)}, u32[]{:S(2)}) collective-permute-start(bf16[192,768]{1,0:T(8,128)(2,1)S(1)} %constant_dynamic-update-slice_fusion.16), channel_id=1, source_target_pairs={{0,1},{1,0},{2,3},{3,2},{4,5},{5,4},{6,7},{7,6},{8,9},{9,8},{10,11... | collective-permute-start | bytes 884744 | tf_op jit(solution)/shard_map/ppermute | solution.py:848
  87.7 29.4 %collective-permute-start.19 = (bf16[672,384]{1,0:T(8,128)(2,1)S(1)}, bf16[672,384]{1,0:T(8,128)(2,1)S(1)}, u32[]{:S(2)}, u32[]{:S(2)}) collective-permute-start(bf16[672,384]{1,0:T(8,128)(2,1)S(1)} %constant_dynamic-update-slice_fusion.2.q1), channel_id=1, source_target_pairs={{0,4},{4,0},{8,12},{12,8},{1,5},{5,1},{9,13},{13,9},{2,6},{6,2},{1... | collective-permute-start | bytes 1548296 | tf_op jit(solution)/shard_map/ppermute | solution.py:848
  116.7 62.3 %collective-permute-start.42 = (bf16[192,768]{1,0:T(8,128)(2,1)}, bf16[192,768]{1,0:T(8,128)(2,1)}, u32[]{:S(2)}, u32[]{:S(2)}) collective-permute-start(bf16[192,768]{1,0:T(8,128)(2,1)} %q0.1), channel_id=1, source_target_pairs={{0,4},{4,0},{8,12},{12,8},{1,5},{5,1},{9,13},{13,9},{2,6},{6,2},{1... | collective-permute-start | bytes 884744 | tf_op jit(solution)/shard_map/ppermute | solution.py:848
  140.1 40.7 %collective-permute-start.39 = (bf16[768,768]{1,0:T(8,128)(2,1)}, bf16[768,768]{1,0:T(8,128)(2,1)}, u32[]{:S(2)}, u32[]{:S(2)}) collective-permute-start(bf16[768,768]{1,0:T(8,128)(2,1)} %constant_dynamic-update-slice_fusion.11.p0), channel_id=1, source_target_pairs={{0,4},{4,0},{8,12},{12,8},{1,5},{5,1},{9,13},{13,9},{2,6},{6,2},{1... | collective-permute-start | bytes 3538952 | tf_op jit(solution)/shard_map/ppermute | solution.py:848
  140.4 37.7 %collective-permute-start.35 = (bf16[768,768]{1,0:T(8,128)(2,1)}, bf16[768,768]{1,0:T(8,128)(2,1)}, u32[]{:S(2)}, u32[]{:S(2)}) collective-permute-start(bf16[768,768]{1,0:T(8,128)(2,1)} %constant_dynamic-update-slice_fusion.11.p0), channel_id=1, source_target_pairs={{0,8},{4,12},{8,0},{12,4},{1,9},{5,13},{9,1},{13,5},{2,10},{6,14},... | collective-permute-start | bytes 3538952 | tf_op jit(solution)/shard_map/ppermute | solution.py:848
  152.7 23.9 %collective-permute-start.41 = (bf16[672,768]{1,0:T(8,128)(2,1)S(1)}, bf16[672,768]{1,0:T(8,128)(2,1)}, u32[]{:S(2)}, u32[]{:S(2)}) collective-permute-start(bf16[672,768]{1,0:T(8,128)(2,1)S(1)} %pad_maximum_fusion.q1), channel_id=1, source_target_pairs={{0,16},{16,0},{1,17},{17,1},{2,18},{18,2},{3,19},{19,3},{4,20},{20... | collective-permute-start | bytes 3096584 | tf_op jit(solution)/shard_map/ppermute | solution.py:848
  157.3 22.3 %collective-permute-start.43 = (bf16[672,768]{1,0:T(8,128)(2,1)S(1)}, bf16[672,768]{1,0:T(8,128)(2,1)}, u32[]{:S(2)}, u32[]{:S(2)}) collective-permute-start(bf16[672,768]{1,0:T(8,128)(2,1)S(1)} %pad_maximum_fusion.q1), channel_id=1, source_target_pairs={{0,4},{4,0},{8,12},{12,8},{1,5},{5,1},{9,13},{13,9},{2,6},{6,2},{1... | collective-permute-start | bytes 3096584 | tf_op jit(solution)/shard_map/ppermute | solution.py:848
  176.7 29.8 %collective-permute-start.44 = (bf16[672,768]{1,0:T(8,128)(2,1)}, bf16[672,768]{1,0:T(8,128)(2,1)}, u32[]{:S(2)}, u32[]{:S(2)}) collective-permute-start(bf16[672,768]{1,0:T(8,128)(2,1)} %collective-permute-done.41.q2), channel_id=1, source_target_pairs={{0,4},{4,0},{8,12},{12,8},{1,5},{5,1},{9,13},{13,9},{2,6},{6,2},{1... | collective-permute-start | bytes 3096584 | tf_op jit(solution)/shard_map/ppermute | solution.py:848
  178.1 28.4 %collective-permute-start.40 = (bf16[768,768]{1,0:T(8,128)(2,1)}, bf16[768,768]{1,0:T(8,128)(2,1)}, u32[]{:S(2)}, u32[]{:S(2)}) collective-permute-start(bf16[768,768]{1,0:T(8,128)(2,1)} %collective-permute-done.35.p2), channel_id=1, source_target_pairs={{0,4},{4,0},{8,12},{12,8},{1,5},{5,1},{9,13},{13,9},{2,6},{6,2},{1... | collective-permute-start | bytes 3538952 | tf_op jit(solution)/shard_map/ppermute | solution.py:848
  179.0 27.4 %collective-permute-start.38 = (bf16[560,384]{1,0:T(8,128)(2,1)S(1)}, bf16[560,384]{1,0:T(8,128)(2,1)S(1)}, u32[]{:S(2)}, u32[]{:S(2)}) collective-permute-start(bf16[560,384]{1,0:T(8,128)(2,1)S(1)} %get-tuple-element.166), channel_id=1, source_target_pairs={{0,12},{4,8},{8,4},{12,0},{1,13},{5,9},{9,5},{13,1},{2,14},{6,10},... | collective-permute-start | bytes 1290248 | tf_op jit(solution)/shard_map/ppermute | solution.py:848
  179.6 26.8 %collective-permute-start.37 = (bf16[560,384]{1,0:T(8,128)(2,1)S(1)}, bf16[560,384]{1,0:T(8,128)(2,1)S(1)}, u32[]{:S(2)}, u32[]{:S(2)}) collective-permute-start(bf16[560,384]{1,0:T(8,128)(2,1)S(1)} %get-tuple-element.167), channel_id=1, source_target_pairs={{0,8},{4,12},{8,0},{12,4},{1,9},{5,13},{9,1},{13,5},{2,10},{6,14},... | collective-permute-start | bytes 1290248 | tf_op jit(solution)/shard_map/ppermute | solution.py:848
  180.9 25.6 %collective-permute-start.36 = (bf16[560,384]{1,0:T(8,128)(2,1)S(1)}, bf16[560,384]{1,0:T(8,128)(2,1)S(1)}, u32[]{:S(2)}, u32[]{:S(2)}) collective-permute-start(bf16[560,384]{1,0:T(8,128)(2,1)S(1)} %get-tuple-element.168), channel_id=1, source_target_pairs={{0,4},{4,0},{8,12},{12,8},{1,5},{5,1},{9,13},{13,9},{2,6},{6,2},{1... | collective-permute-start | bytes 1290248 | tf_op jit(solution)/shard_map/ppermute | solution.py:848
  255.7 49.4 %collective-permute-start.47 = (bf16[560,384]{1,0:T(8,128)(2,1)S(1)}, bf16[560,384]{1,0:T(8,128)(2,1)S(1)}, u32[]{:S(2)}, u32[]{:S(2)}) collective-permute-start(bf16[560,384]{1,0:T(8,128)(2,1)S(1)} %get-tuple-element.162), channel_id=1, source_target_pairs={{0,12},{4,8},{8,4},{12,0},{1,13},{5,9},{9,5},{13,1},{2,14},{6,10},... | collective-permute-start | bytes 1290248 | tf_op jit(solution)/shard_map/ppermute | solution.py:848
  256.0 49.1 %collective-permute-start.46 = (bf16[560,384]{1,0:T(8,128)(2,1)S(1)}, bf16[560,384]{1,0:T(8,128)(2,1)S(1)}, u32[]{:S(2)}, u32[]{:S(2)}) collective-permute-start(bf16[560,384]{1,0:T(8,128)(2,1)S(1)} %get-tuple-element.163), channel_id=1, source_target_pairs={{0,8},{4,12},{8,0},{12,4},{1,9},{5,13},{9,1},{13,5},{2,10},{6,14},... | collective-permute-start | bytes 1290248 | tf_op jit(solution)/shard_map/ppermute | solution.py:848
  257.2 47.8 %collective-permute-start.45 = (bf16[560,384]{1,0:T(8,128)(2,1)S(1)}, bf16[560,384]{1,0:T(8,128)(2,1)S(1)}, u32[]{:S(2)}, u32[]{:S(2)}) collective-permute-start(bf16[560,384]{1,0:T(8,128)(2,1)S(1)} %get-tuple-element.164), channel_id=1, source_target_pairs={{0,4},{4,0},{8,12},{12,8},{1,5},{5,1},{9,13},{13,9},{2,6},{6,2},{1... | collective-permute-start | bytes 1290248 | tf_op jit(solution)/shard_map/ppermute | solution.py:848
  339.9 20.6 %collective-permute-start.52 = (bf16[560,384]{1,0:T(8,128)(2,1)S(1)}, bf16[560,384]{1,0:T(8,128)(2,1)S(1)}, u32[]{:S(2)}, u32[]{:S(2)}) collective-permute-start(bf16[560,384]{1,0:T(8,128)(2,1)S(1)} %get-tuple-element.159), channel_id=1, source_target_pairs={{0,8},{4,12},{8,0},{12,4},{1,9},{5,13},{9,1},{13,5},{2,10},{6,14},... | collective-permute-start | bytes 1290248 | tf_op jit(solution)/shard_map/ppermute | solution.py:848
  (84 other events, 1152.7 us)
where the time goes:
time: 380 us; the launch traced here: 372 us
  Pallas kernels  203 us (53%)
  starting transfers between devices  78 us (21%)
  waiting for transfers between devices  61.9 us (16%)
  local copies, waits for them, and re-layouts  24.8 us (7%)
    ppermute x61, starting transfers between devices, flip(): return lax.ppermute(values, axis, [(i, i ^ distance) for i in range(size)])  78 us
    ppermute x61, waiting for transfers between devices, flip(): return lax.ppermute(values, axis, [(i, i ^ distance) for i in range(size)])  61.9 us
    pallas_call x1, Pallas kernels, attention_back(): pl.pallas_call(attention_back_kernel, out_shape=(s(ROWS, 3 * D, dtype=BF)...  47.2 us
    pallas_call x1, Pallas kernels, mlp(): pl.pallas_call(mlp_kernel, out_shape=(s(4, HALF, 2 * QUART, dtype=BF), s(...  45.9 us
    pallas_call x3, Pallas kernels, attention(): pl.pallas_call(functools.partial(attention_kernel, kinds=PARTS[part]), ou...  41.9 us
    pallas_call x1, Pallas kernels, token_grad(): pl.pallas_call(token_grad_kernel, out_shape=jax.ShapeDtypeStruct((4, HALF...  14.6 us
    unnamed x111, local copies, waits for them, and re-layouts  12.3 us
    pallas_call x1, Pallas kernels, qkv_rows(): pl.pallas_call(qkv_kernel, out_shape=(s(ROWS, D), s(ROWS, D)) + tuple((s(...  10.6 us
  transfers between devices with their start and end apart: 61, of which 13 were waited for; matrix products, arithmetic and copies ran while one was open for 4% of the time, Pallas kernels for 36%

commit v1 on v0

--- a/solution.py
+++ b/solution.py
@@ -92,103 +92,81 @@
     return pl.CostEstimate(flops=int(us * 9e8), transcendentals=0, bytes_accessed=0)
 
 
-def place_window(kind, count, shift, width, spare=-100000):
+def place_window(kind, count, moved, width, spare=-100000):
     row = lax.broadcasted_iota(jnp.int32, (count, width), 0)
     lane = lax.broadcasted_iota(jnp.int32, (count, width), 1)
     if kind in (RIGHT, CORNER):
         src = (row // EDGE) * WIN + row % EDGE
     else:
         src = jnp.where(row < SLOTS, row, spare)
-    return (lane == src + shift).astype(F32).astype(BF)
-
-
-def window_list(dest):
-    items = [(FULL, FULLR * j, NWIN * dest + j) for j in range(4)]
-    items.append((RIGHT, OFFS[1], NWIN * dest + 4))
-    items.append((BOTTOM, OFFS[2], NWIN * 4 + dest))
-    if dest == 3:
-        items.append((CORNER, OFFS[3], NWIN * NWIN - 1))
-    return items
-
-
-def span_of(window):
-    start = SLOTS * window
+    return (lane == src + moved).astype(F32).astype(BF)
+
+
+SPAN = 384
+LAST = SLOTS * (NWIN * NWIN - 1)
+LAST_LOW = LAST // 128 * 128
+
+
+def window_span(window):
+    start = window * SLOTS
     low = start // 128 * 128
-    high = min(-(-(start + SLOTS) // 128) * 128, IMG_TOK)
-    return low, high, start - low
-
-
-def pack_kernel(where_ref, x_ref, out_ref, rows_ref, *, spare):
-    mine = where_ref[0]
-    for dest in range(4):
-        if dest != 3:
-            rows_ref[OFFS[3] :, :] = jnp.zeros((CORNR, QUART), BF)
-        for kind, offset, window in window_list(dest):
-            low, high, moved = span_of(window)
-            pick = place_window(kind, NQ[kind], moved, high - low, spare)
-            rows_ref[offset : offset + NQ[kind], :] = nt(pick, x_ref[:, low:high]).astype(BF)
+    return pl.ds(pl.multiple_of(low, 128), SPAN), start - low
+
+
+def each_window(dest, visit):
+    def full(j, carry):
+        visit(FULL, pl.multiple_of(FULLR * j, 16), NWIN * dest + j)
+        return carry
+
+    lax.fori_loop(0, 4, full, 0)
+    visit(RIGHT, OFFS[1], NWIN * dest + 4)
+    visit(BOTTOM, OFFS[2], NWIN * 4 + dest)
+
+
+def pack_rows(mine, x_ref, rows_ref, spare):
+    def one(dest, carry):
         slot = jnp.bitwise_xor(mine, dest)
-        out_ref[slot, :, :QUART] = rows_ref[:HALF, :]
-        out_ref[slot, :, QUART:] = rows_ref[HALF:, :]
-
-
-def pack(where, x, spare=-100000):
-    return pl.pallas_call(
-        functools.partial(pack_kernel, spare=spare),
-        out_shape=jax.ShapeDtypeStruct((4, HALF, 2 * QUART), BF),
+
+        def visit(kind, offset, window):
+            span, moved = window_span(window)
+            pick = place_window(kind, NQ[kind], moved, SPAN, spare)
+            rows_ref[slot, pl.ds(offset, NQ[kind]), :] = nt(pick, x_ref[:, span]).astype(BF)
+
+        each_window(dest, visit)
+        rows_ref[slot, OFFS[3] :, :] = jnp.zeros((CORNR, QUART), BF)
+        return carry
+
+    lax.fori_loop(0, 4, one, 0)
+    pick = place_window(CORNER, CORNR, LAST - LAST_LOW, IMG_TOK - LAST_LOW)
+    rows_ref[jnp.bitwise_xor(mine, 3), OFFS[3] :, :] = nt(pick, x_ref[:, LAST_LOW:]).astype(BF)
+
+
+def pack_kernel(where_ref, x_ref, o0, o1, o2, o3, rows_ref):
+    pack_rows(where_ref[0], x_ref, rows_ref, -100000)
+    for slot, out in enumerate((o0, o1, o2, o3)):
+        out[:, :QUART] = rows_ref[slot, :HALF, :]
+        out[:, QUART:] = rows_ref[slot, HALF:, :]
+
+
+PIECE = jax.ShapeDtypeStruct((HALF, 2 * QUART), BF)
+
+
+def pack(where, x):
+    return pl.pallas_call(
+        pack_kernel,
+        out_shape=(PIECE,) * 4,
         in_specs=[sm(), vm()],
-        out_specs=vm(),
-        scratch_shapes=[pltpu.VMEM((ROWS, QUART), BF)],
+        out_specs=[vm()] * 4,
+        scratch_shapes=[pltpu.VMEM((4, ROWS, QUART), BF)],
         compiler_params=params(),
         cost_estimate=cost(4),
         name="pack",
     )(where, x)
 
 
-def unpack_kernel(where_ref, y0, y1, y2, y3, out_ref, acc_ref, rows_ref):
-    mine = where_ref[0]
-    acc_ref[...] = jnp.zeros_like(acc_ref)
-    for slot, y in enumerate((y0, y1, y2, y3)):
-        rows_ref[slot, :HALF, :] = y[:, :QUART]
-        rows_ref[slot, HALF:, :] = y[:, QUART:]
-    for source in range(4):
-        slot = jnp.bitwise_xor(mine, source)
-        for kind, offset, window in window_list(source):
-            low, high, moved = span_of(window)
-            pick = place_window(kind, NQ[kind], moved, high - low)
-            acc_ref[:, low:high] += tn(rows_ref[slot, offset : offset + NQ[kind], :], pick)
-    out_ref[...] = acc_ref[:, :IMG_TOK].astype(out_ref.dtype)
-
-
-def unpack(where, pieces, dtype):
-    return pl.pallas_call(
-        unpack_kernel,
-        out_shape=jax.ShapeDtypeStruct((QUART, IMG_TOK), dtype),
-        in_specs=[sm()] + [vm()] * 4,
-        out_specs=vm(),
-        scratch_shapes=[
-            pltpu.VMEM((QUART, -(-IMG_TOK // 128) * 128), F32),
-            pltpu.VMEM((4, ROWS, QUART), BF),
-        ],
-        compiler_params=params(),
-        cost_estimate=cost(4),
-        name="unpack",
-    )(where, *pieces)
-
-
-def join_pieces(pieces, dst_ref):
-    for slot, piece in enumerate(pieces):
-        dst_ref[:HALF, QUART * slot : QUART * (slot + 1)] = piece[:, :QUART]
-        dst_ref[HALF:, QUART * slot : QUART * (slot + 1)] = piece[:, QUART:]
-
-
-def split_pieces(src_ref, out_ref):
-    for slot in range(4):
-        out_ref[slot, :, :QUART] = src_ref[:HALF, QUART * slot : QUART * (slot + 1)]
-        out_ref[slot, :, QUART:] = src_ref[HALF:, QUART * slot : QUART * (slot + 1)]
-
-
-def weight_pack_kernel(where_ref, qkv_w, proj_w, alpha_ref, beta_ref, alpha_half, beta_half):
+def front_kernel(
+    where_ref, x_ref, qkv_w, proj_w, o0, o1, o2, o3, alpha_ref, beta_ref, alpha_half, beta_half, rows_ref,
+):
     heads = qkv_w.shape[1] // (3 * HD)
     for h in range(heads):
         for t in range(3):
@@ -198,46 +176,115 @@
     rows = pl.ds(pl.multiple_of(where_ref[1] * HBLK, 32), HBLK)
     alpha_half[...] = alpha_ref[rows, :]
     beta_half[...] = beta_ref[rows, :]
-
-
-def weight_pack(where, qkv_w, proj_w):
+    pack_rows(where_ref[0], x_ref, rows_ref, 0)
+    for slot, out in enumerate((o0, o1, o2, o3)):
+        out[:, :QUART] = rows_ref[slot, :HALF, :]
+        out[:, QUART:] = rows_ref[slot, HALF:, :]
+
+
+def front(where, x, qkv_w, proj_w):
     s = lambda *shape: jax.ShapeDtypeStruct(shape, BF)
     return pl.pallas_call(
-        weight_pack_kernel,
-        out_shape=(s(QUART, 2 * QUART), s(QUART, 2 * QUART), s(HBLK, 2 * QUART), s(HBLK, 2 * QUART)),
-        in_specs=[sm(), vm(), vm()],
-        out_specs=[vm()] * 4,
-        compiler_params=params(),
-        cost_estimate=cost(2),
-        name="weight_pack",
-    )(where, qkv_w, proj_w)
+        front_kernel,
+        out_shape=(PIECE,) * 4
+        + (s(QUART, 2 * QUART), s(QUART, 2 * QUART), s(HBLK, 2 * QUART), s(HBLK, 2 * QUART)),
+        in_specs=[sm(), vm(), vm(), vm()],
+        out_specs=[vm()] * 8,
+        scratch_shapes=[pltpu.VMEM((4, ROWS, QUART), BF)],
+        compiler_params=params(),
+        cost_estimate=cost(5),
+        name="token_and_weight_pack",
+    )(where, x, qkv_w, proj_w)
+
+
+def unpack_kernel(where_ref, *refs, bounds):
+    pieces, (out_ref, acc_ref, rows_ref) = refs[:-3], refs[-3:]
+    mine = where_ref[0]
+    acc_ref[...] = jnp.zeros_like(acc_ref)
+    index = 0
+    for low, high in bounds:
+        half = (high - low) // 2
+        for slot in range(4):
+            piece = pieces[index]
+            rows_ref[slot, low : low + half, :] = piece[:, :QUART]
+            rows_ref[slot, low + half : high, :] = piece[:, QUART:]
+            index += 1
+
+    def one(source, carry):
+        slot = jnp.bitwise_xor(mine, source)
+
+        def visit(kind, offset, window):
+            span, moved = window_span(window)
+            pick = place_window(kind, NQ[kind], moved, SPAN)
+            acc_ref[:, span] += tn(rows_ref[slot, pl.ds(offset, NQ[kind]), :], pick)
+
+        each_window(source, visit)
+        return carry
+
+    lax.fori_loop(0, 4, one, 0)
+    pick = place_window(CORNER, CORNR, LAST - LAST_LOW, IMG_TOK - LAST_LOW)
+    acc_ref[:, LAST_LOW:IMG_TOK] += tn(rows_ref[jnp.bitwise_xor(mine, 3), OFFS[3] :, :], pick)
+    out_ref[...] = acc_ref[:, :IMG_TOK].astype(out_ref.dtype)
+
+
+def unpack(where, pieces, dtype, bounds=((0, ROWS),)):
+    return pl.pallas_call(
+        functools.partial(unpack_kernel, bounds=bounds),
+        out_shape=jax.ShapeDtypeStruct((QUART, IMG_TOK), dtype),
+        in_specs=[sm()] + [vm()] * len(pieces),
+        out_specs=vm(),
+        scratch_shapes=[
+            pltpu.VMEM((QUART, -(-IMG_TOK // 128) * 128), F32),
+            pltpu.VMEM((4, ROWS, QUART), BF),
+        ],
+        compiler_params=params(),
+        cost_estimate=cost(4),
+        name="unpack",
+    )(where, *pieces)
+
+
+def join_pieces(pieces, dst_ref):
+    for slot, piece in enumerate(pieces):
+        dst_ref[:HALF, QUART * slot : QUART * (slot + 1)] = piece[:, :QUART]
+        dst_ref[HALF:, QUART * slot : QUART * (slot + 1)] = piece[:, QUART:]
+
+
+def split_pieces(src_ref, outs):
+    half = src_ref.shape[0] // 2
+    for slot, out in enumerate(outs):
+        out[:, :QUART] = src_ref[:half, QUART * slot : QUART * (slot + 1)]
+        out[:, QUART:] = src_ref[half:, QUART * slot : QUART * (slot + 1)]
 
 
 def adapter_pack_kernel(
-    pick_ref, qkv_up, proj_dn, fc1_up, fc2_dn, qkv_dn, fc1_dn, proj_up, fc2_up, send_ref, row_ref,
+    pick_ref, qkv_up, proj_dn, fc1_up, fc2_dn, qkv_dn, fc1_dn, proj_up, fc2_up, gain1, gain2,
+    s0, s1, s2, s3, row_ref,
 ):
     heads = qkv_up.shape[2] // (3 * HD)
-    for j in range(4):
+    for j, send_ref in enumerate((s0, s1, s2, s3)):
         a = pick_ref[j]
         for h in range(heads):
             for t in range(3):
-                send_ref[j, :RANK, QUART * t + HD * h : QUART * t + HD * (h + 1)] = qkv_up[
+                send_ref[:RANK, QUART * t + HD * h : QUART * t + HD * (h + 1)] = qkv_up[
                     a, :, HD * (3 * h + t) : HD * (3 * h + t + 1)
                 ]
-        send_ref[j, :RANK, 3 * QUART :] = proj_dn[a]
-        send_ref[j, RANK : 2 * RANK, :] = fc1_up[a]
-        send_ref[j, 2 * RANK :, :] = fc2_dn[a]
+        send_ref[:RANK, 3 * QUART :] = proj_dn[a]
+        send_ref[RANK : 2 * RANK, :] = fc1_up[a]
+        send_ref[2 * RANK :, :] = fc2_dn[a]
     for i, ref in enumerate((qkv_dn, fc1_dn, proj_up, fc2_up)):
-        row_ref[:, QUART * i : QUART * (i + 1)] = ref[pick_ref[0]]
+        row_ref[:RANK, QUART * i : QUART * (i + 1)] = ref[pick_ref[0]]
+    for i, ref in enumerate((gain1, gain2)):
+        row_ref[RANK:, QUART * i : QUART * (i + 1)] = jnp.broadcast_to(ref[...], (RANK, QUART))
+    row_ref[RANK:, 2 * QUART :] = jnp.zeros((RANK, 2 * QUART), BF)
 
 
 def adapter_pack(pick, *mats):
     s = lambda *shape: jax.ShapeDtypeStruct(shape, BF)
     return pl.pallas_call(
         adapter_pack_kernel,
-        out_shape=(s(4, 3 * RANK, D), s(RANK, D)),
-        in_specs=[sm()] + [vm()] * 8,
-        out_specs=[vm()] * 2,
+        out_shape=(s(3 * RANK, D),) * 4 + (s(2 * RANK, D),),
+        in_specs=[sm()] + [vm()] * 10,
+        out_specs=[vm()] * 5,
         compiler_params=params(),
         cost_estimate=cost(2),
         name="adapter_pack",
@@ -272,7 +319,7 @@
 
 def prep1_kernel(
     where_ref, p0, p1, p2, p3, q0, q1, q2, q3, q4, q5, r0, r1, r2, r3, a0, a1, a2, a3,
-    wqkv_ref, wproj_ref, dqkv, uqkv, dproj, uproj, d1, u1, d2, u2,
+    wqkv_ref, wproj_ref, dqkv, uqkv, dproj, uproj, d1, u1, d2, u2, gain1, gain2,
 ):
     half = where_ref[1]
     for j, a in enumerate((a0, a1, a2, a3)):
@@ -283,7 +330,9 @@
         d2[:, D * j : D * (j + 1)] = a[2 * RANK :, :]
     for k, ref in enumerate((r0, r1, r2, r3)):
         for i, dst in enumerate((dqkv, d1, uproj, u2)):
-            dst[:, QUART * k : QUART * (k + 1)] = ref[:, QUART * i : QUART * (i + 1)]
+            dst[:, QUART * k : QUART * (k + 1)] = ref[:RANK, QUART * i : QUART * (i + 1)]
+        for i, dst in enumerate((gain1, gain2)):
+            dst[:, QUART * k : QUART * (k + 1)] = ref[RANK : RANK + 1, QUART * i : QUART * (i + 1)].astype(F32)
     alpha, beta = (p0, p1, p2, p3), (q0, q1, q2, q3, q4, q5)
     for k in range(4):
         for j in range(4):
@@ -317,9 +366,10 @@
         out_shape=(
             s(D, 3 * D), s(D, D), s(RANK, D), s(RANK, 3 * D), s(RANK, D), s(RANK, D),
             s(RANK, D), s(RANK, 4 * D), s(RANK, 4 * D), s(RANK, D),
+            jax.ShapeDtypeStruct((1, D), F32), jax.ShapeDtypeStruct((1, D), F32),
         ),
         in_specs=[sm()] + [vm()] * 18,
-        out_specs=[vm()] * 10,
+        out_specs=[vm()] * 12,
         compiler_params=params(),
         cost_estimate=cost(7),
         name="attention_weights",
@@ -360,12 +410,12 @@
     return lax.broadcasted_iota(jnp.int32, (KEYS, 128), 0) < SLOTS
 
 
-UNROLL = 6
-UNROLL_BACK = 6
+GROUP = 6
+GROUP_BACK = 6
 
 
 def pair_columns(pair):
-    return tuple(pl.ds(pl.multiple_of(D * t + 128 * pair, 128), 128) for t in range(3))
+    return tuple(slice(D * t + 128 * pair, D * t + 128 * (pair + 1)) for t in range(3))
 
 
 def attend_window(kind, row0, qkv_ref, att_ref, exp_ref, inv_ref, rel_ref, shift_ref, keys_ref):
@@ -376,38 +426,44 @@
     ones = jnp.where(live, 1.0, 0.0).astype(BF)
     amount = shift_ref[kind, :count, :]
     onehot = keys_ref[kind]
-
-    def one_pair(pair, carry):
-        cols, kcols, vcols = pair_columns(pair)
-        q_tile = qkv_ref[rows, cols]
-        k_tile = pad_rows(qkv_ref[rows, kcols] * BF(HD**-0.5))
-        v_tile = pad_rows(qkv_ref[rows, vcols])
-        if kind == FULL:
-            v_tile = jnp.where(live, v_tile, 0).astype(BF)
-        rel = barrel(nn(q_tile, rel_ref[...]), amount, True).astype(BF)
-        both = []
-        for odd in range(2):
+    rel_mat = rel_ref[...]
+    for first in range(0, D // 128, GROUP):
+        pairs = range(first, first + GROUP)
+        heads = [(pair, odd) for pair in pairs for odd in range(2)]
+        q_tile = {p: qkv_ref[rows, pair_columns(p)[0]] for p in pairs}
+        rel = {p: nn(q_tile[p], rel_mat) for p in pairs}
+        rel = {p: barrel(rel[p], amount, True).astype(BF) for p in pairs}
+        k_tile = {p: pad_rows(qkv_ref[rows, pair_columns(p)[1]] * BF(HD**-0.5)) for p in pairs}
+        scores = {}
+        for p, odd in heads:
             if odd:
-                q_aug, k_aug = jnp.where(low_q, rel, q_tile), jnp.where(low_k, onehot, k_tile)
-                v_aug = jnp.where(low_k, ones, v_tile)
+                q_aug, k_aug = jnp.where(low_q, rel[p], q_tile[p]), jnp.where(low_k, onehot, k_tile[p])
             else:
-                q_aug, k_aug = jnp.where(low_q, q_tile, rel), jnp.where(low_k, k_tile, onehot)
-                v_aug = jnp.where(low_k, v_tile, ones)
-            scores = nt(q_aug, k_aug)
-            exponent = jnp.exp(scores - jnp.max(scores, axis=1, keepdims=True)).astype(BF)
-            exp_ref[2 * pair + odd, rows, :] = exponent
-            both.append(nn(exponent, v_aug))
-        inverse = 1.0 / pltpu.roll(jnp.where(low_q, both[1], both[0]), HD, 1)
-        inv_ref[rows, cols] = inverse
-        att_ref[rows, cols] = (jnp.where(low_q, both[0], both[1]) * inverse).astype(BF)
-        return carry
-
-    lax.fori_loop(0, D // 128, one_pair, 0, unroll=UNROLL)
+                q_aug, k_aug = jnp.where(low_q, q_tile[p], rel[p]), jnp.where(low_k, k_tile[p], onehot)
+            scores[p, odd] = nt(q_aug, k_aug)
+        top = {h: jnp.max(scores[h], axis=1, keepdims=True) for h in heads}
+        exponent = {h: jnp.exp(scores[h] - top[h]).astype(BF) for h in heads}
+        both = {}
+        for p, odd in heads:
+            exp_ref[2 * p + odd, rows, :] = exponent[p, odd]
+            v_tile = pad_rows(qkv_ref[rows, pair_columns(p)[2]])
+            if kind == FULL:
+                v_tile = jnp.where(live, v_tile, 0).astype(BF)
+            v_aug = jnp.where(low_k, ones, v_tile) if odd else jnp.where(low_k, v_tile, ones)
+            both[p, odd] = nn(exponent[p, odd], v_aug)
+        for p in pairs:
+            cols = pair_columns(p)[0]
+            inverse = 1.0 / pltpu.roll(jnp.where(low_q, both[p, 1], both[p, 0]), HD, 1)
+            inv_ref[rows, cols] = inverse
+            att_ref[rows, cols] = (jnp.where(low_q, both[p, 0], both[p, 1]) * inverse).astype(BF)
 
 
 PARTS = ((FULL, FULL), (FULL, FULL), (RIGHT, BOTTOM, CORNER))
 PART_ROWS = tuple(sum(NQ[kind] for kind in part) for part in PARTS)
 PART_OFFS = (0, PART_ROWS[0], PART_ROWS[0] + PART_ROWS[1])
+
+
+TAIL = ((0, 576), (576, ROWS))
 
 
 def qkv_kernel(x0, x1, x2, x3, gain_ref, wqkv_ref, x_ref, hid_ref, qkv_a, qkv_b, qkv_c):
@@ -492,12 +548,13 @@
 
 
 CHUNK = 512
+LOCK = 2
 
 
 def mlp_kernel(
     where_ref, middle_ref, g0, g1, g2, g3, gain_ref,
     p0, p1, p2, p3, q0, q1, q2, q3, q4, q5, d1, u1, d2, u2,
-    out_ref, gmid_ref, down1, up1, down2, up2,
+    o0, o1, o2, o3, gmid_ref, down1, up1, down2, up2,
     gm_ref, out_rows, h2_ref, acc_mlp, acc_gh, gu1, ad2, w1_ref, w2_ref, sem,
 ):
     half = where_ref[1]
@@ -547,24 +604,29 @@
         ad2[...] = jnp.zeros_like(ad2)
 
         def chunk_step(c, inner_carry):
-            cols = pl.ds(pl.multiple_of(c * CHUNK, CHUNK), CHUNK)
-            w1 = w1_ref[:, cols]
-            w2 = w2_ref[:, cols]
-            inner = nn(h2_ref[...], w1)
-            gact = nn(gm_ref[rows, :], w2)
-            half = 0.5 * (1.0 + lax.erf(inner * 2**-0.5))
-            act = (inner * half).astype(BF)
-            slope = half + inner * (jnp.exp(-0.5 * inner * inner) * (2 * np.pi) ** -0.5)
-            ginner = (gact * slope).astype(BF)
-            acc_mlp[...] += nt(act, w2)
-            acc_gh[...] += nt(ginner, w1)
-            up1[:, cols] += nn(ad1, ginner)
-            gu1[...] += nt(u1[:, cols], ginner)
-            ad2[...] += nt(d2[:, cols], act)
-            down2[:, cols] += nn(gu2, act)
+            spans = [
+                pl.ds(pl.multiple_of((c * LOCK + i) * CHUNK, CHUNK), CHUNK) for i in range(LOCK)
+            ]
+            h2 = h2_ref[...]
+            gm = gm_ref[rows, :]
+            inner = [nn(h2, w1_ref[:, span]) for span in spans]
+            gact = [nn(gm, w2_ref[:, span]) for span in spans]
+            act, ginner = [], []
+            for i in range(LOCK):
+                half = 0.5 * (1.0 + lax.erf(inner[i] * 2**-0.5))
+                act.append((inner[i] * half).astype(BF))
+                slope = half + inner[i] * (jnp.exp(-0.5 * inner[i] * inner[i]) * (2 * np.pi) ** -0.5)
+                ginner.append((gact[i] * slope).astype(BF))
+            for i, span in enumerate(spans):
+                acc_mlp[...] += nt(act[i], w2_ref[:, span])
+                acc_gh[...] += nt(ginner[i], w1_ref[:, span])
+                up1[:, span] += nn(ad1, ginner[i])
+                gu1[...] += nt(u1[:, span], ginner[i])
+                ad2[...] += nt(d2[:, span], act[i])
+                down2[:, span] += nn(gu2, act[i])
             return inner_carry
 
-        lax.fori_loop(0, 4 * D // CHUNK, chunk_step, 0)
+        lax.fori_loop(0, 4 * D // (CHUNK * LOCK), chunk_step, 0)
         down1[...] += nn(gu1[...].astype(BF), h2_ref[...])
         up2[...] += nn(ad2[...].astype(BF), gm_ref[rows, :])
         middle = middle_ref[rows, :]
@@ -574,19 +636,17 @@
         return carry
 
     lax.fori_loop(0, 2, tile_step, 0)
-    split_pieces(out_rows, out_ref)
+    split_pieces(out_rows, (o0, o1, o2, o3))
 
 
 def mlp(where, middle, pieces, gain, alpha, beta, d1, u1, d2, u2):
     s = lambda *shape, dtype=F32: jax.ShapeDtypeStruct(shape, dtype)
     return pl.pallas_call(
         mlp_kernel,
-        out_shape=(
-            s(4, HALF, 2 * QUART, dtype=BF), s(ROWS, D),
-            s(RANK, D), s(RANK, 4 * D), s(RANK, 4 * D), s(RANK, D),
-        ),
+        out_shape=(PIECE,) * 4
+        + (s(ROWS, D), s(RANK, D), s(RANK, 4 * D), s(RANK, 4 * D), s(RANK, D)),
         in_specs=[sm()] + [vm()] * 6 + [pl.BlockSpec(memory_space=pl.ANY)] * 10 + [vm()] * 4,
-        out_specs=[vm()] * 6,
+        out_specs=[vm()] * 9,
         scratch_shapes=[
             pltpu.VMEM((ROWS, D), BF), pltpu.VMEM((ROWS, D), BF), pltpu.VMEM((HALF, D), BF),
             pltpu.VMEM((HALF, D), F32), pltpu.VMEM((HALF, D), F32),
@@ -615,44 +675,48 @@
     ).astype(BF)
     amount = shift_ref[kind, :count, :]
     onehot = keys_ref[kind]
-
-    def one_pair(pair, carry):
-        cols, kcols, vcols = pair_columns(pair)
-        q_tile = qkv_ref[rows, cols]
-        k_tile = pad_rows(qkv_ref[rows, kcols] * BF(HD**-0.5))
-        v_tile = pad_rows(qkv_ref[rows, vcols])
-        if kind == FULL:
-            v_tile = jnp.where(live, v_tile, 0).astype(BF)
-        go_tile = (gatt_ref[rows, cols].astype(F32) * inv_ref[rows, cols]).astype(BF)
-        delta = nn((go_tile.astype(F32) * att_ref[rows, cols].astype(F32)).astype(BF), across)
-        high = delta.astype(BF)
-        rest = (delta - high.astype(F32)).astype(BF)
-        delta = jnp.where(lane_q == 0, high, jnp.where(lane_q == 1, rest, 0)).astype(BF)
-        q_t = q_tile.T
-        go_t = go_tile.T
-        gq, gk, gv = [], [], []
-        for odd in range(2):
-            if odd:
-                go_aug, v_aug = jnp.where(low_q, delta, go_tile), jnp.where(low_k, ones, v_tile)
-                k_aug = jnp.where(low_k, onehot, k_tile)
-            else:
-                go_aug, v_aug = jnp.where(low_q, go_tile, delta), jnp.where(low_k, v_tile, ones)
-                k_aug = jnp.where(low_k, k_tile, onehot)
-            exponent = exp_ref[2 * pair + odd, rows, :]
-            gs = (exponent.astype(F32) * nt(go_aug, v_aug)).astype(BF)
-            side = slice(HD * odd, HD * (odd + 1))
-            gv.append(nn(go_t[side, :], exponent))
-            gk.append(nn(q_t[side, :], gs))
-            gq.append(nn(gs, k_aug))
-        sums = barrel(jnp.where(low_q, gq[1], gq[0]), amount, False).astype(BF)
-        gqkv_ref[rows, cols] = (jnp.where(low_q, gq[0], gq[1]) + nt(sums, rel_ref[...])).astype(BF)
-        gk_tile = (jnp.concatenate(gk, axis=0) * HD**-0.5).astype(BF).T
-        gv_tile = jnp.concatenate(gv, axis=0).astype(BF).T
-        gqkv_ref[rows, kcols] = gk_tile[:count, :]
-        gqkv_ref[rows, vcols] = gv_tile[:count, :]
-        return carry
-
-    lax.fori_loop(0, D // 128, one_pair, 0, unroll=UNROLL_BACK)
+    rel_mat = rel_ref[...]
+    for first in range(0, D // 128, GROUP_BACK):
+        pairs = range(first, first + GROUP_BACK)
+        heads = [(pair, odd) for pair in pairs for odd in range(2)]
+        go_tile = {
+            p: (gatt_ref[rows, pair_columns(p)[0]].astype(F32) * inv_ref[rows, pair_columns(p)[0]]).astype(BF)
+            for p in pairs
+        }
+        delta = {
+            p: nn((go_tile[p].astype(F32) * att_ref[rows, pair_columns(p)[0]].astype(F32)).astype(BF), across)
+            for p in pairs
+        }
+        go_t = {p: go_tile[p].T for p in pairs}
+        gv = {}
+        for p, odd in heads:
+            gv[p, odd] = nn(go_t[p][HD * odd : HD * (odd + 1), :], exp_ref[2 * p + odd, rows, :])
+        gscore = {}
+        for p in pairs:
+            high = delta[p].astype(BF)
+            rest = (delta[p] - high.astype(F32)).astype(BF)
+            low_delta = jnp.where(lane_q == 0, high, jnp.where(lane_q == 1, rest, 0)).astype(BF)
+            v_tile = pad_rows(qkv_ref[rows, pair_columns(p)[2]])
+            if kind == FULL:
+                v_tile = jnp.where(live, v_tile, 0).astype(BF)
+            gscore[p, 0] = nt(jnp.where(low_q, go_tile[p], low_delta), jnp.where(low_k, v_tile, ones))
+            gscore[p, 1] = nt(jnp.where(low_q, low_delta, go_tile[p]), jnp.where(low_k, ones, v_tile))
+        q_t = {p: qkv_ref[rows, pair_columns(p)[0]].T for p in pairs}
+        gs = {(p, odd): (exp_ref[2 * p + odd, rows, :].astype(F32) * gscore[p, odd]).astype(BF) for p, odd in heads}
+        gk = {(p, odd): nn(q_t[p][HD * odd : HD * (odd + 1), :], gs[p, odd]) for p, odd in heads}
+        gq = {}
+        for p in pairs:
+            k_tile = pad_rows(qkv_ref[rows, pair_columns(p)[1]] * BF(HD**-0.5))
+            gq[p, 0] = nn(gs[p, 0], jnp.where(low_k, k_tile, onehot))
+            gq[p, 1] = nn(gs[p, 1], jnp.where(low_k, onehot, k_tile))
+        sums = {p: barrel(jnp.where(low_q, gq[p, 1], gq[p, 0]), amount, False).astype(BF) for p in pairs}
+        for p in pairs:
+            cols, kcols, vcols = pair_columns(p)
+            gv_tile = jnp.concatenate([gv[p, 0], gv[p, 1]], axis=0).astype(BF).T
+            gqkv_ref[rows, vcols] = gv_tile[:count, :]
+            gk_tile = (jnp.concatenate([gk[p, 0], gk[p, 1]], axis=0) * HD**-0.5).astype(BF).T
+            gqkv_ref[rows, kcols] = gk_tile[:count, :]
+            gqkv_ref[rows, cols] = (jnp.where(low_q, gq[p, 0], gq[p, 1]) + nt(sums[p], rel_mat)).astype(BF)
 
 
 def attention_back_kernel(
@@ -702,35 +766,54 @@
     )(gmid, hid, *qkvs, *atts, *exps, *invs, wproj, rel, shift, keys, dqkv, uqkv, dproj, uproj)
 
 
-def token_grad_kernel(gmid_ref, x_ref, gqkv_ref, gain_ref, wqkv_ref, out_ref, gh_ref, out_rows):
+def token_grad_kernel(gmid_hbm, x_hbm, gqkv_hbm, gain_ref, wqkv_ref, o0, o1, o2, o3,
+                      gmid_ref, x_ref, gqkv_ref, gh_ref, out_rows, sem, *, low, high):
+    span = pl.ds(low, high - low)
+    copies = [
+        pltpu.make_async_copy(src.at[span, :], dst, sem.at[i])
+        for i, (src, dst) in enumerate(((gqkv_hbm, gqkv_ref), (x_hbm, x_ref), (gmid_hbm, gmid_ref)))
+    ]
+    for copy in copies:
+        copy.start()
+    copies[0].wait()
     gh_ref[...] = nt(gqkv_ref[...], wqkv_ref[...])
+    copies[1].wait()
+    copies[2].wait()
     gain = gain_ref[...]
 
     def norm_step(i, carry):
-        rows = pl.ds(pl.multiple_of(i * 112, 16), 112)
+        rows = pl.ds(pl.multiple_of(i * TAIL_STEP, 16), TAIL_STEP)
         normed, inv_std = normalize(x_ref[rows, :].astype(F32))
         back = norm_back(gh_ref[rows, :] * gain, normed, inv_std)
         out_rows[rows, :] = (gmid_ref[rows, :] + back).astype(BF)
         return carry
 
-    lax.fori_loop(0, ROWS // 112, norm_step, 0)
-    split_pieces(out_rows, out_ref)
-
-
-def token_grad(gmid, x, gqkv, gain, wqkv):
-    return pl.pallas_call(
-        token_grad_kernel,
-        out_shape=jax.ShapeDtypeStruct((4, HALF, 2 * QUART), BF),
-        in_specs=[vm()] * 5,
-        out_specs=vm(),
-        scratch_shapes=[pltpu.VMEM((ROWS, D), F32), pltpu.VMEM((ROWS, D), BF)],
-        compiler_params=params(),
-        cost_estimate=cost(14),
+    lax.fori_loop(0, (high - low) // TAIL_STEP, norm_step, 0)
+    split_pieces(out_rows, (o0, o1, o2, o3))
+
+
+TAIL_STEP = 32
+
+
+def token_grad(gmid, x, gqkv, gain, wqkv, low, high):
+    count = high - low
+    hbm = pl.BlockSpec(memory_space=pl.ANY)
+    return pl.pallas_call(
+        functools.partial(token_grad_kernel, low=low, high=high),
+        out_shape=(jax.ShapeDtypeStruct((count // 2, 2 * QUART), BF),) * 4,
+        in_specs=[hbm, hbm, hbm, vm(), vm()],
+        out_specs=[vm()] * 4,
+        scratch_shapes=[
+            pltpu.VMEM((count, D), F32), pltpu.VMEM((count, D), BF), pltpu.VMEM((count, 3 * D), BF),
+            pltpu.VMEM((count, D), F32), pltpu.VMEM((count, D), BF), pltpu.SemaphoreType.DMA((3,)),
+        ],
+        compiler_params=params(),
+        cost_estimate=cost(8),
         name="token_gradient",
     )(gmid, x, gqkv, gain, wqkv)
 
 
-def grad_pack_kernel(where_ref, down_q, up_q, down_p, up_p, down1, up1, down2, up2, out_ref, buf_ref):
+def grad_pack_kernel(where_ref, down_q, up_q, down_p, up_p, down1, up1, down2, up2, o0, o1, o2, o3, buf_ref):
     mine = where_ref[0]
     for k in range(4):
         for i, ref in enumerate((down_q, down1, up_p, up2)):
@@ -747,15 +830,16 @@
             buf_ref[k, base : base + 4, 3 * QUART :] = down_p[ranks, QUART * j : QUART * (j + 1)]
             buf_ref[k, base + 4 : base + 8, :] = up1[ranks, D * j : D * (j + 1)]
             buf_ref[k, base + 8 : base + 12, :] = down2[ranks, D * j : D * (j + 1)]
-    out_ref[...] = buf_ref[...].astype(BF)
+    for k, out in enumerate((o0, o1, o2, o3)):
+        out[...] = buf_ref[k].astype(BF)
 
 
 def grad_pack(where, *grads):
     return pl.pallas_call(
         grad_pack_kernel,
-        out_shape=jax.ShapeDtypeStruct((4, 4 * RANK, D), BF),
+        out_shape=(jax.ShapeDtypeStruct((4 * RANK, D), BF),) * 4,
         in_specs=[sm()] + [vm()] * 8,
-        out_specs=vm(),
+        out_specs=[vm()] * 4,
         scratch_shapes=[pltpu.VMEM((4, 4 * RANK, D), F32)],
         compiler_params=params(),
         cost_estimate=cost(2),
@@ -763,21 +847,21 @@
     )(where, *grads)
 
 
-def grad_sum_kernel(g0, g1, g2, g3, out_ref, buf_ref):
+def grad_sum_kernel(g0, g1, g2, g3, o0, o1, o2, o3, buf_ref):
     total = g0[...].astype(F32) + g1[...].astype(F32) + g2[...].astype(F32) + g3[...].astype(F32)
     buf_ref[...] = jnp.zeros_like(buf_ref)
-    for j in range(4):
-        buf_ref[:RANK, :] = total[:RANK, :]
+    buf_ref[:RANK, :] = total[:RANK, :]
+    for j, out in enumerate((o0, o1, o2, o3)):
         buf_ref[RANK : RANK + 12, :] = total[RANK + 12 * j : RANK + 12 * (j + 1), :]
-        out_ref[j] = buf_ref[...].astype(BF)
+        out[...] = buf_ref[...].astype(BF)
 
 
 def grad_sum(pieces):
     return pl.pallas_call(
         grad_sum_kernel,
-        out_shape=jax.ShapeDtypeStruct((4, 2 * RANK, D), BF),
+        out_shape=(jax.ShapeDtypeStruct((2 * RANK, D), BF),) * 4,
         in_specs=[vm()] * 4,
-        out_specs=vm(),
+        out_specs=[vm()] * 4,
         scratch_shapes=[pltpu.VMEM((2 * RANK, D), F32)],
         compiler_params=params(),
         cost_estimate=cost(2),
@@ -901,67 +985,76 @@
     rel = rel_matrix(rel_h, rel_w)
     shift, keys = jnp.asarray(SHIFT_NP), jnp.asarray(KEYS_NP)
 
-    alpha_own, beta_own, alpha_half, beta_half = weight_pack(where, qkv_weight, proj_weight)
+    *token_slots, alpha_own, beta_own, alpha_half, beta_half = front(where, tokens, qkv_weight, proj_weight)
     b0 = flip(beta_half, "row", 2)
     alpha_near = col_halves(alpha_half)
-    token_slots = pack(where, tokens, 0)
     x_pieces = exchange(token_slots, "row")
     beta_near = col_pairs(beta_half, b0)
     alpha_far = flip(alpha_near, "dp", 1)
     g = jnp.concatenate([alpha_own, alpha_near, alpha_far], axis=0)
-    g, _ = after((g, x_pieces[1]), x_pieces[2])
+    g, *x_pieces = after((g, *x_pieces))
     gy = flip(g, "row", 2)
     beta_far = flip(beta_near, "dp", 1)
-    beta1 = [beta_own, beta_near, beta_far] + [flip(m, "row", 1) for m in (beta_own, beta_near, beta_far)]
-
-    gains = jnp.stack([norm1_gain, norm2_gain]).astype(F32)
-    send, row_adapters = adapter_pack(
+
+    *send, row_adapters = adapter_pack(
         pick, qkv_up, swap(proj_down), fc1_up, swap(fc2_down), swap(qkv_down), swap(fc1_down), proj_up, fc2_up,
+        norm1_gain.reshape(1, -1), norm2_gain.reshape(1, -1),
     )
-    gains, send, row_adapters = after((gains, send, row_adapters), beta_near)
+    *send, row_adapters = after((*send, row_adapters), alpha_near)
     col_adapters = exchange(send, "col")
-    gain_all = jnp.concatenate(exchange([gains] * 4, "row"), axis=1)
-    gain1, gain2 = gain_all[0:1], gain_all[1:2]
     row_adapters = exchange([row_adapters] * 4, "row")
 
     fc1_half = lax.dynamic_slice_in_dim(fc1_weight, half * HBLK, HBLK, 0)
     fc2_half = lax.dynamic_slice_in_dim(fc2_weight, half * HBLK, HBLK, 0)
+    fc1_half, fc2_half = after((fc1_half, fc2_half), *col_adapters)
+    fc1_near = [flip(fc1_half, "col", j) for j in range(1, 4)]
     c0 = flip(fc2_half, "row", 2)
-    fc1_half, fc2_half, c0 = after((fc1_half, fc2_half, c0), col_adapters[1], col_adapters[2], col_adapters[3])
-    fc1_near = col_halves(fc1_half)
-    fc2_near = col_pairs(fc2_half, c0)
+    grad_slots = pack(where, grad_out)
+
+    alpha1 = [g, flip(g, "row", 1), gy, flip(gy, "row", 1)]
+    beta1 = [beta_own, beta_near, beta_far] + [flip(m, "row", 1) for m in (beta_own, beta_near, beta_far)]
+    wqkv, wproj, dqkv, uqkv, dproj, uproj, d1, u1, d2, u2, gain1, gain2 = prep1(
+        where, alpha1, beta1, row_adapters, col_adapters
+    )
+    *grad_slots, wqkv = after((*grad_slots, wqkv), c0)
+    g_pieces = exchange(grad_slots, "row")
+    fc2_two = after((jnp.concatenate([fc2_half, c0], axis=0),), wqkv)[0]
+    fc2_near = [flip(fc2_two, "col", j) for j in range(1, 4)]
+    fc1_near = after(tuple(fc1_near), wqkv)
+    fc1_near = jnp.concatenate(fc1_near, axis=0)
     fc1_far = flip(fc1_near, "dp", 1)
+    x, hid, *qkvs = qkv_rows(x_pieces, gain1, wqkv)
+    *qkvs, fc1_far = after((*qkvs, fc1_far))
     h = jnp.concatenate([fc1_weight, fc1_near, fc1_far], axis=0)
-
-    grad_slots = pack(where, grad_out)
-    alpha1 = [g, flip(g, "row", 1), gy, flip(gy, "row", 1)]
-    wqkv, wproj, dqkv, uqkv, dproj, uproj, d1, u1, d2, u2 = prep1(where, alpha1, beta1, row_adapters, col_adapters)
-    x, hid, *qkvs = qkv_rows(x_pieces, gain1, wqkv)
-    qkv0, h = after((qkvs[0], h), gy)
     hy = flip(h, "row", 2)
-    part0 = attention(0, qkv0, rel, shift, keys)
-    qkv1, fc2_near = after((qkvs[1], fc2_near), part0[0])
+    part0 = attention(0, qkvs[0], rel, shift, keys)
+    qkv1, *fc2_near = after((qkvs[1], *fc2_near), part0[0])
+    fc2_near = jnp.concatenate([c0] + fc2_near, axis=0)
     fc2_far = flip(fc2_near, "dp", 1)
     part1 = attention(1, qkv1, rel, shift, keys)
-    qkv2, hy, grad_slots = after((qkvs[2], hy, grad_slots), part1[0])
-    g_pieces = exchange(grad_slots, "row")
+    qkv2, hy = after((qkvs[2], hy), part1[0])
     alpha2 = [h, flip(h, "row", 1), hy, flip(hy, "row", 1)]
     part2 = attention(2, qkv2, rel, shift, keys)
     atts, exps, invs = zip(part0, part1, part2)
     middle = project(x, atts, wproj)
+    middle, fc2_far, *g_pieces = after((middle, fc2_far, *g_pieces))
     beta2 = [fc2_weight, fc2_near, fc2_far] + [flip(m, "row", 1) for m in (fc2_weight, fc2_near, fc2_far)]
 
-    out_slots, gmid, down1, up1, down2, up2 = mlp(where, middle, g_pieces, gain2, alpha2, beta2, d1, u1, d2, u2)
+    *out_slots, gmid, down1, up1, down2, up2 = mlp(where, middle, g_pieces, gain2, alpha2, beta2, d1, u1, d2, u2)
     out_pieces = exchange(out_slots, "row")
     gqkv, down_q, up_q, down_p, up_p = attention_back(
         gmid, hid, qkvs, atts, exps, invs, wproj, rel, shift, keys, dqkv, uqkv, dproj, uproj
     )
     gqkv, down_q, up_q, down_p, up_p = after((gqkv, down_q, up_q, down_p, up_p), *out_pieces)
     packed = grad_pack(where, down_q, up_q, down_p, up_p, down1, up1, down2, up2)
+    *packed, gqkv = after((*packed, gqkv))
     row_sums = exchange(packed, "row")
-    back_slots = token_grad(gmid, x, gqkv, gain1, wqkv)
-    back_slots, *row_sums = after((back_slots, *row_sums))
-    back_pieces = exchange(back_slots, "row")
+    back0 = token_grad(gmid, x, gqkv, gain1, wqkv, *TAIL[0])
+    *row_sums, gqkv = after((*row_sums, gqkv), back0[0])
+    back_pieces = exchange(back0, "row")
+    back1 = token_grad(gmid, x, gqkv, gain1, wqkv, *TAIL[1])
+    *row_sums, = after(tuple(row_sums), back1[0])
+    back_pieces += exchange(back1, "row")
     summed = grad_sum(row_sums)
     images = jnp.stack(exchange(summed, "col"))
     step = 1
@@ -972,7 +1065,7 @@
     rests = [rest] + [flip(rest, "row", k) for k in range(1, 4)]
     qkv_upg, proj_dn, fc1_upg, fc2_dn = grad_join(where, rests)
     result = unpack(where, out_pieces, BF)
-    grad_tokens = unpack(where, back_pieces, F32)
+    grad_tokens = unpack(where, back_pieces, F32, TAIL)
     return (
         result, grad_tokens,
         swap(qkv_dn), qkv_upg, swap(proj_dn), proj_upg, swap(fc1_dn), fc1_upg, swap(fc2_dn), fc2_upg,

time: 380 us -> 354 us (0.932)
  the two profiles are of different devices: /device:TPU:1 before, /device:TPU:0 now
where the time goes in v1:
time: 354 us; the launch traced here: 347 us
  Pallas kernels  188 us (53%)
  waiting for transfers between devices  81.2 us (23%)
  starting transfers between devices  57.3 us (16%)
  local copies, waits for them, and re-layouts  15.3 us (4%)
    ppermute x61, waiting for transfers between devices, flip(): return lax.ppermute(values, axis, [(i, i ^ distance) for i in range(size)])  81.2 us
    ppermute x61, starting transfers between devices, flip(): return lax.ppermute(values, axis, [(i, i ^ distance) for i in range(size)])  57.3 us
    pallas_call x1, Pallas kernels, mlp(): pl.pallas_call(mlp_kernel, out_shape=(PIECE,) * 4 + (s(ROWS, D), s(RANK,...  45.3 us
    pallas_call x1, Pallas kernels, attention_back(): pl.pallas_call(attention_back_kernel, out_shape=(s(ROWS, 3 * D, dtype=BF)...  27 us
    pallas_call x2, Pallas kernels, token_grad(): pl.pallas_call(functools.partial(token_grad_kernel, low=low, high=high),...  23.6 us
    pallas_call x3, Pallas kernels, attention(): pl.pallas_call(functools.partial(attention_kernel, kinds=PARTS[part]), ou...  23 us
    pallas_call x2, Pallas kernels, unpack(): pl.pallas_call(functools.partial(unpack_kernel, bounds=bounds), out_shape...  17.8 us
    unnamed x123, local copies, waits for them, and re-layouts  11.7 us
  transfers between devices with their start and end apart: 61, of which 18 were waited for; matrix products, arithmetic and copies ran while one was open for 4% of the time, Pallas kernels for 37%

profile of v1, /device:TPU:0, one launch (start us, length us, event | category | flops | bytes accessed | tf_op | source)
XLA Modules:
  0.0 347.0 jit_solution(16771625746005371092)
XLA Ops:
  1.3 8.6 %token_and_weight_pack.1 = (bf16[560,384]{1,0:T(8,128)(2,1)}, bf16[560,384]{1,0:T(8,128)(2,1)}, bf16[560,384]{1,0:T(8,128)(2,1)}, bf16[560,384]{1,0:T(8,128)(2,1...) custom-call(s32[2]{0:T(128)} %pad_add_fusion.where_ref, ...), custom_call_target="tpu_custom_call" | custom-call | flops 4499999744 | tf_op jit(solution)/shard_map/token_and_weight_pack/pallas_call | solution.py:187
  9.9 5.0 %collective-permute-start.2 = (bf16[96,384]{1,0:T(8,128)(2,1)}, bf16[96,384]{1,0:T(8,128)(2,1)S(1)}, u32[]{:S(2)}, u32[]{:S(2)}) collective-permute-start(bf16[96,384]{1,0:T(8,128)(2,1)} %get-tuple-element.149), channel_id=1, source_target_pairs={{0,3},{1,2},{2,1},{3,0},{4,7},{5,6},{6,5},{7,4},{8,11},{9,10},{10,... | collective-permute-start | bytes 221192 | tf_op jit(solution)/shard_map/ppermute | solution.py:932
  35.6 6.9 %collective-permute-done.6.x3 = bf16[560,384]{1,0:T(8,128)(2,1)S(1)} collective-permute-done((bf16[560,384]{1,0:T(8,128)(2,1)}, bf16[560,384]{1,0:T(8,128)(2,1)S(1)}, u32[]{:S(2)}, u32[]{:S(2)}) %collective-permute-start.6) | collective-permute-done | bytes 430112 | tf_op jit(solution)/shard_map/ppermute | solution.py:932
  46.5 8.0 %pack.1 = (bf16[560,384]{1,0:T(8,128)(2,1)}, bf16[560,384]{1,0:T(8,128)(2,1)}, bf16[560,384]{1,0:T(8,128)(2,1)}, bf16[560,384]{1,0:T(8,128)(2,1)}) custom-call(s32[2]{0:T(128)} %pad_add_fusion.where_ref, bf16[192,4900]{1,0:T(8,128)(2,1)} %x_ref.3), custom_call_target="tpu_custom_call" | custom-call | flops 3600000000 | tf_op jit(solution)/shard_map/pack/pallas_call | solution.py:155
  59.0 3.7 %collective-permute-start.22 = (bf16[48,768]{1,0:T(8,128)(2,1)S(1)}, bf16[48,768]{1,0:T(8,128)(2,1)S(1)}, u32[]{:S(2)}, u32[]{:S(2)}) collective-permute-start(bf16[48,768]{1,0:T(8,128)(2,1)S(1)} %copy-done.42), channel_id=1, source_target_pairs={{0,2},{1,3},{2,0},{3,1},{4,6},{5,7},{6,4},{7,5},{8,10},{9,11},{10,... | collective-permute-start | bytes 221192 | tf_op jit(solution)/shard_map/ppermute | solution.py:932
  70.8 4.7 %collective-permute-done.24 = bf16[96,768]{1,0:T(8,128)(2,1)S(1)} collective-permute-done((bf16[96,768]{1,0:T(8,128)(2,1)S(1)}, bf16[96,768]{1,0:T(8,128)(2,1)S(1)}, u32[]{:S(2)}, u32[]{:S(2)}) %collective-permute-start.24) | collective-permute-done | bytes 147488 | tf_op jit(solution)/shard_map/ppermute | solution.py:932
  76.9 3.4 collective-permute-start.27
  82.1 7.4 %attention_weights.1 = (bf16[768,2304]{1,0:T(8,128)(2,1)}, bf16[768,768]{1,0:T(8,128)(2,1)}, bf16[16,768]{1,0:T(8,128)(2,1)}, bf16[16,2304]{1,0:T(8,128)(2,1)}, ...) custom-call(s32[2]{0:T(128)} %pad_add_fusion.where_ref, ...), custom_call_target="tpu_custom_call" | custom-call | flops 6300000256 | tf_op jit(solution)/shard_map/attention_weights/pallas_call | solution.py:364
  89.5 3.5 collective-permute-start.31
  94.0 12.1 %collective-permute-done.26 = bf16[96,768]{1,0:T(8,128)(2,1)S(1)} collective-permute-done((bf16[96,768]{1,0:T(8,128)(2,1)S(1)}, bf16[96,768]{1,0:T(8,128)(2,1)S(1)}, u32[]{:S(2)}, u32[]{:S(2)}) %collective-permute-start.26) | collective-permute-done | bytes 147488 | tf_op jit(solution)/shard_map/ppermute | solution.py:932
  107.5 10.8 %norm_and_qkv.1 = (bf16[1120,768]{1,0:T(8,128)(2,1)}, bf16[1120,768]{1,0:T(8,128)(2,1)}, bf16[416,2304]{1,0:T(8,128)(2,1)}, bf16[416,2304]{1,0:T(8,128)(2,1)}, bf16[288,2304]{1,0:T(8,128)(2,1)}) custom-call(bf16[560,384]{1,0:T(8,128)(2,1)} %get-tuple-element.154.x0, bf16[560,384]{1,0:T(8,128)(2,1)} %copy-done.13, bf16[560,384]{1,0:T(8,128)(2,1)} %copy-done.14, ...), custom_call_target="tpu_custom_call" | custom-call | flops 10800000000 | tf_op jit(solution)/shard_map/norm_and_qkv/pallas_call | solution.py:491
  119.2 7.9 %attention_forward.3 = (bf16[416,768]{1,0:T(8,128)(2,1)}, bf16[12,416,208]{2,1,0:T(8,128)(2,1)}, f32[416,768]{1,0:T(8,128)}) custom-call(bf16[416,2304]{1,0:T(8,128)(2,1)} %get-tuple-element.187.qkv_ref.qkv_a, bf16[128,128]{1,0:T(8,128)(2,1)} %fusion.2.rel_ref, s32[4,208,128]{2,1,0:T(8,128)} %constant.40.clone.shift_ref, ...), custom_call_target="tpu_custom_call" | custom-call | flops 8999999488 | tf_op jit(solution)/shard_map/attention_forward/pallas_call | solution.py:521
  131.6 8.1 %attention_forward.4 = (bf16[416,768]{1,0:T(8,128)(2,1)}, bf16[12,416,208]{2,1,0:T(8,128)(2,1)}, f32[416,768]{1,0:T(8,128)}) custom-call(bf16[416,2304]{1,0:T(8,128)(2,1)} %get-tuple-element.191.qkv_ref.qkv_b, bf16[128,128]{1,0:T(8,128)(2,1)} %fusion.2.rel_ref, s32[4,208,128]{2,1,0:T(8,128)} %constant.40.clone.shift_ref, ...), custom_call_target="tpu_custom_call" | custom-call | flops 8999999488 | tf_op jit(solution)/shard_map/attention_forward/pallas_call | solution.py:521
  139.6 25.6 %collective-permute-done.32.p2 = bf16[768,768]{1,0:T(8,128)(2,1)} collective-permute-done((bf16[768,768]{1,0:T(8,128)(2,1)S(1)}, bf16[768,768]{1,0:T(8,128)(2,1)}, u32[]{:S(2)}, u32[]{:S(2)}) %collective-permute-start.32) | collective-permute-done | bytes 1179680 | tf_op jit(solution)/shard_map/ppermute | solution.py:932
  166.4 7.1 %attention_forward.5 = (bf16[288,768]{1,0:T(8,128)(2,1)}, bf16[12,288,208]{2,1,0:T(8,128)(2,1)}, f32[288,768]{1,0:T(8,128)}) custom-call(bf16[288,2304]{1,0:T(8,128)(2,1)} %get-tuple-element.195.qkv_ref.qkv_c, bf16[128,128]{1,0:T(8,128)(2,1)} %fusion.2.rel_ref, s32[4,208,128]{2,1,0:T(8,128)} %constant.40.clone.shift_ref, ...), custom_call_target="tpu_custom_call" | custom-call | flops 8999999488 | tf_op jit(solution)/shard_map/attention_forward/pallas_call | solution.py:521
  173.5 5.6 %projection.1.middle_ref = f32[1120,768]{1,0:T(8,128)} custom-call(bf16[1120,768]{1,0:T(8,128)(2,1)} %get-tuple-element.179.x_ref.x_hbm, bf16[416,768]{1,0:T(8,128)(2,1)} %get-tuple-element.188.att_a, bf16[416,768]{1,0:T(8,128)(2,1)} %get-tuple-element.192.att_b, bf16[288,768]{1,0:T(8,128)(2,1)} %get-tuple-element.196.att_c, ...), custom_call_target="tpu_custom_call" | custom-call | flops 4499999744 | tf_op jit(solution)/shard_map/projection/pallas_call | solution.py:539
  179.6 10.4 %collective-permute-done.33.q2 = bf16[672,768]{1,0:T(8,128)(2,1)} collective-permute-done((bf16[672,768]{1,0:T(8,128)(2,1)S(1)}, bf16[672,768]{1,0:T(8,128)(2,1)}, u32[]{:S(2)}, u32[]{:S(2)}) %collective-permute-start.33) | collective-permute-done | bytes 1032224 | tf_op jit(solution)/shard_map/ppermute | solution.py:932
  194.7 45.3 %mlp_forward_backward.1 = (bf16[560,384]{1,0:T(8,128)(2,1)}, bf16[560,384]{1,0:T(8,128)(2,1)}, bf16[560,384]{1,0:T(8,128)(2,1)}, bf16[560,384]{1,0:T(8,128)(2,1)...) custom-call(s32[2]{0:T(128)} %pad_add_fusion.where_ref, ...), custom_call_target="tpu_custom_call" | custom-call | flops 43200000000 | tf_op jit(solution)/shard_map/mlp_forward_backward/pallas_call | solution.py:644
  242.0 27.0 %attention_backward.1 = (bf16[1120,2304]{1,0:T(8,128)(2,1)}, f32[16,768]{1,0:T(8,128)}, f32[16,2304]{1,0:T(8,128)}, f32[16,768]{1,0:T(8,128)}, f32[16,768]{1,0:T(8,128)}) custom-call(f32[1120,768]{1,0:T(8,128)} %get-tuple-element.221.gmid_ref.gmid_hbm, bf16[1120,768]{1,0:T(8,128)(2,1)} %get-tuple-element.222.hid_ref, ...), custom_call_target="tpu_custom_call" | custom-call | flops 40499998720 | tf_op jit(solution)/shard_map/attention_backward/pallas_call | solution.py:757
  273.8 12.0 %token_gradient.2 = (bf16[288,384]{1,0:T(8,128)(2,1)}, bf16[288,384]{1,0:T(8,128)(2,1)}, bf16[288,384]{1,0:T(8,128)(2,1)}, bf16[288,384]{1,0:T(8,128)(2,1)}) custom-call(f32[1120,768]{1,0:T(8,128)} %get-tuple-element.221.gmid_ref.gmid_hbm, bf16[1120,768]{1,0:T(8,128)(2,1)} %get-tuple-element.179.x_ref.x_hbm, bf16[1120,2304]{1,0:T(8,128)(2,1)} %get-tuple-element.260.gqkv_hbm, ...), custom_call_target="tpu_custom_call" | custom-call | flops 7200000000 | tf_op jit(solution)/shard_map/token_gradient/pallas_call | solution.py:801
  287.8 8.5 %unpack.2 = bf16[192,4900]{1,0:T(8,128)(2,1)} custom-call(s32[2]{0:T(128)} %pad_add_fusion.where_ref, bf16[560,384]{1,0:T(8,128)(2,1)} %get-tuple-element.217.refs_0_, bf16[560,384]{1,0:T(8,128)(2,1)} %copy-done.16, bf16[560,384]{1,0:T(8,128)(2,1)} %copy-done.17, bf16[560,384]{1,0:T(8,128)(2,1)} %copy-done.18), custom_call_target="tpu_custom_call" | custom-call | flops 3600000000 | tf_op jit(solution)/shard_map/unpack/pallas_call | solution.py:231
  296.4 11.6 %token_gradient.3 = (bf16[272,384]{1,0:T(8,128)(2,1)}, bf16[272,384]{1,0:T(8,128)(2,1)}, bf16[272,384]{1,0:T(8,128)(2,1)}, bf16[272,384]{1,0:T(8,128)(2,1)}) custom-call(f32[1120,768]{1,0:T(8,128)} %get-tuple-element.221.gmid_ref.gmid_hbm, bf16[1120,768]{1,0:T(8,128)(2,1)} %get-tuple-element.179.x_ref.x_hbm, bf16[1120,2304]{1,0:T(8,128)(2,1)} %get-tuple-element.260.gqkv_hbm, ...), custom_call_target="tpu_custom_call" | custom-call | flops 7200000000 | tf_op jit(solution)/shard_map/token_gradient/pallas_call | solution.py:801
  322.0 3.6 %collective-permute-done.57 = bf16[4,32,768]{2,1,0:T(8,128)(2,1)S(1)} collective-permute-done((bf16[4,32,768]{2,1,0:T(8,128)(2,1)S(1)}, bf16[4,32,768]{2,1,0:T(8,128)(2,1)S(1)}, u32[]{:S(2)}, u32[]{:S(2)}) %collective-permute-start.57) | collective-permute-done | bytes 196640 | tf_op jit(solution)/shard_map/ppermute | solution.py:932
  333.4 9.3 %unpack.3 = f32[192,4900]{1,0:T(8,128)} custom-call(s32[2]{0:T(128)} %pad_add_fusion.where_ref, bf16[288,384]{1,0:T(8,128)(2,1)} %get-tuple-element.252.refs_0_, bf16[288,384]{1,0:T(8,128)(2,1)} %copy-done.20, bf16[288,384]{1,0:T(8,128)(2,1)} %copy-done.21, bf16[288,384]{1,0:T(8,128)(2,1)} %copy-done.23, bf16[272,384]{1,0:T(8,128)(2,1)} %get-tuple-element.261.refs_4_, ...), custom_call_target="tpu_custom_call" | custom-call | flops 3600000000 | tf_op jit(solution)/shard_map/unpack/pallas_call | solution.py:231
  (266 shorter events, 89.1 us)
Async XLA Ops:
  17.2 18.3 %collective-permute-start.4 = (bf16[560,384]{1,0:T(8,128)(2,1)}, bf16[560,384]{1,0:T(8,128)(2,1)S(1)}, u32[]{:S(2)}, u32[]{:S(2)}) collective-permute-start(bf16[560,384]{1,0:T(8,128)(2,1)} %get-tuple-element.151), channel_id=1, source_target_pairs={{0,4},{4,0},{8,12},{12,8},{1,5},{5,1},{9,13},{13,9},{2,6},{6,2},{1... | collective-permute-start | bytes 1290248 | tf_op jit(solution)/shard_map/ppermute | solution.py:932
  21.6 20.9 %collective-permute-start.6 = (bf16[560,384]{1,0:T(8,128)(2,1)}, bf16[560,384]{1,0:T(8,128)(2,1)S(1)}, u32[]{:S(2)}, u32[]{:S(2)}) collective-permute-start(bf16[560,384]{1,0:T(8,128)(2,1)} %get-tuple-element.153), channel_id=1, source_target_pairs={{0,12},{4,8},{8,4},{12,0},{1,13},{5,9},{9,5},{13,1},{2,14},{6,10},... | collective-permute-start | bytes 1290248 | tf_op jit(solution)/shard_map/ppermute | solution.py:932
  42.5 21.6 %collective-permute-start.8 = (bf16[768,384]{1,0:T(8,128)(2,1)S(1)}, bf16[768,384]{1,0:T(8,128)(2,1)}, u32[]{:S(2)}, u32[]{:S(2)}) collective-permute-start(bf16[768,384]{1,0:T(8,128)(2,1)S(1)} %constant_dynamic-update-slice_fusion.3.p0), channel_id=1, source_target_pairs={{0,8},{4,12},{8,0},{12,4},{1,9},{5,13},{9,1},{13,5},{2,10},{6,14},... | collective-permute-start | bytes 1769480 | tf_op jit(solution)/shard_map/ppermute | solution.py:932
  45.9 23.1 %collective-permute-start.14 = (bf16[672,384]{1,0:T(8,128)(2,1)}, bf16[672,384]{1,0:T(8,128)(2,1)}, u32[]{:S(2)}, u32[]{:S(2)}) collective-permute-start(bf16[672,384]{1,0:T(8,128)(2,1)} %constant_dynamic-update-slice_fusion.10.q1), channel_id=1, source_target_pairs={{0,16},{16,0},{1,17},{17,1},{2,18},{18,2},{3,19},{19,3},{4,20},{20... | collective-permute-start | bytes 1548296 | tf_op jit(solution)/shard_map/ppermute | solution.py:932
  80.3 25.7 %collective-permute-start.26 = (bf16[96,768]{1,0:T(8,128)(2,1)S(1)}, bf16[96,768]{1,0:T(8,128)(2,1)S(1)}, u32[]{:S(2)}, u32[]{:S(2)}) collective-permute-start(bf16[96,768]{1,0:T(8,128)(2,1)S(1)} %constant_dynamic-slice_fusion.1), channel_id=1, source_target_pairs={{0,2},{1,3},{2,0},{3,1},{4,6},{5,7},{6,4},{7,5},{8,10},{9,11},{10,... | collective-permute-start | bytes 442376 | tf_op jit(solution)/shard_map/ppermute | solution.py:932
  80.3 25.7 %collective-permute-start.25 = (bf16[96,768]{1,0:T(8,128)(2,1)S(1)}, bf16[96,768]{1,0:T(8,128)(2,1)S(1)}, u32[]{:S(2)}, u32[]{:S(2)}) collective-permute-start(bf16[96,768]{1,0:T(8,128)(2,1)S(1)} %constant_dynamic-slice_fusion.1), channel_id=1, source_target_pairs={{0,1},{1,0},{2,3},{3,2},{4,5},{5,4},{6,7},{7,6},{8,9},{9,8},{10,11... | collective-permute-start | bytes 442376 | tf_op jit(solution)/shard_map/ppermute | solution.py:932
  89.5 37.6 %collective-permute-start.31 = (bf16[192,768]{1,0:T(8,128)(2,1)S(1)}, bf16[192,768]{1,0:T(8,128)(2,1)S(1)}, u32[]{:S(2)}, u32[]{:S(2)}) collective-permute-start(bf16[192,768]{1,0:T(8,128)(2,1)S(1)} %pad_maximum_fusion.1), channel_id=1, source_target_pairs={{0,3},{1,2},{2,1},{3,0},{4,7},{5,6},{6,5},{7,4},{8,11},{9,10},{10,... | collective-permute-start | bytes 884744 | tf_op jit(solution)/shard_map/ppermute | solution.py:932
  93.0 35.0 %collective-permute-start.30 = (bf16[192,768]{1,0:T(8,128)(2,1)S(1)}, bf16[192,768]{1,0:T(8,128)(2,1)S(1)}, u32[]{:S(2)}, u32[]{:S(2)}) collective-permute-start(bf16[192,768]{1,0:T(8,128)(2,1)S(1)} %pad_maximum_fusion.1), channel_id=1, source_target_pairs={{0,2},{1,3},{2,0},{3,1},{4,6},{5,7},{6,4},{7,5},{8,10},{9,11},{10,... | collective-permute-start | bytes 884744 | tf_op jit(solution)/shard_map/ppermute | solution.py:932
  93.0 35.9 %collective-permute-start.29 = (bf16[192,768]{1,0:T(8,128)(2,1)S(1)}, bf16[192,768]{1,0:T(8,128)(2,1)S(1)}, u32[]{:S(2)}, u32[]{:S(2)}) collective-permute-start(bf16[192,768]{1,0:T(8,128)(2,1)S(1)} %pad_maximum_fusion.1), channel_id=1, source_target_pairs={{0,1},{1,0},{2,3},{3,2},{4,5},{5,4},{6,7},{7,6},{8,9},{9,8},{10,11... | collective-permute-start | bytes 884744 | tf_op jit(solution)/shard_map/ppermute | solution.py:932
  106.0 67.4 %collective-permute-start.34 = (bf16[560,384]{1,0:T(8,128)(2,1)}, bf16[560,384]{1,0:T(8,128)(2,1)}, u32[]{:S(2)}, u32[]{:S(2)}) collective-permute-start(bf16[560,384]{1,0:T(8,128)(2,1)} %get-tuple-element.202), channel_id=1, source_target_pairs={{0,4},{4,0},{8,12},{12,8},{1,5},{5,1},{9,13},{13,9},{2,6},{6,2},{1... | collective-permute-start | bytes 1290248 | tf_op jit(solution)/shard_map/ppermute | solution.py:932
  118.7 60.4 %collective-permute-start.35 = (bf16[560,384]{1,0:T(8,128)(2,1)}, bf16[560,384]{1,0:T(8,128)(2,1)}, u32[]{:S(2)}, u32[]{:S(2)}) collective-permute-start(bf16[560,384]{1,0:T(8,128)(2,1)} %get-tuple-element.203), channel_id=1, source_target_pairs={{0,8},{4,12},{8,0},{12,4},{1,9},{5,13},{9,1},{13,5},{2,10},{6,14},... | collective-permute-start | bytes 1290248 | tf_op jit(solution)/shard_map/ppermute | solution.py:932
  127.1 52.5 %collective-permute-start.36 = (bf16[560,384]{1,0:T(8,128)(2,1)}, bf16[560,384]{1,0:T(8,128)(2,1)}, u32[]{:S(2)}, u32[]{:S(2)}) collective-permute-start(bf16[560,384]{1,0:T(8,128)(2,1)} %get-tuple-element.204), channel_id=1, source_target_pairs={{0,12},{4,8},{8,4},{12,0},{1,13},{5,9},{9,5},{13,1},{2,14},{6,10},... | collective-permute-start | bytes 1290248 | tf_op jit(solution)/shard_map/ppermute | solution.py:932
  128.0 64.7 %collective-permute-start.37 = (bf16[768,768]{1,0:T(8,128)(2,1)S(1)}, bf16[768,768]{1,0:T(8,128)(2,1)}, u32[]{:S(2)}, u32[]{:S(2)}) collective-permute-start(bf16[768,768]{1,0:T(8,128)(2,1)S(1)} %constant_dynamic-update-slice_fusion.14.p0), channel_id=1, source_target_pairs={{0,4},{4,0},{8,12},{12,8},{1,5},{5,1},{9,13},{13,9},{2,6},{6,2},{1... | collective-permute-start | bytes 3538952 | tf_op jit(solution)/shard_map/ppermute | solution.py:932
  128.9 36.4 %collective-permute-start.32 = (bf16[768,768]{1,0:T(8,128)(2,1)S(1)}, bf16[768,768]{1,0:T(8,128)(2,1)}, u32[]{:S(2)}, u32[]{:S(2)}) collective-permute-start(bf16[768,768]{1,0:T(8,128)(2,1)S(1)} %constant_dynamic-update-slice_fusion.14.p0), channel_id=1, source_target_pairs={{0,8},{4,12},{8,0},{12,4},{1,9},{5,13},{9,1},{13,5},{2,10},{6,14},... | collective-permute-start | bytes 3538952 | tf_op jit(solution)/shard_map/ppermute | solution.py:932
  165.3 24.7 %collective-permute-start.33 = (bf16[672,768]{1,0:T(8,128)(2,1)S(1)}, bf16[672,768]{1,0:T(8,128)(2,1)}, u32[]{:S(2)}, u32[]{:S(2)}) collective-permute-start(bf16[672,768]{1,0:T(8,128)(2,1)S(1)} %copy-done.4), channel_id=1, source_target_pairs={{0,16},{16,0},{1,17},{17,1},{2,18},{18,2},{3,19},{19,3},{4,20},{20... | collective-permute-start | bytes 3096584 | tf_op jit(solution)/shard_map/ppermute | solution.py:932
  173.5 19.8 %collective-permute-start.38 = (bf16[768,768]{1,0:T(8,128)(2,1)}, bf16[768,768]{1,0:T(8,128)(2,1)S(1)}, u32[]{:S(2)}, u32[]{:S(2)}) collective-permute-start(bf16[768,768]{1,0:T(8,128)(2,1)} %collective-permute-done.32.p2), channel_id=1, source_target_pairs={{0,4},{4,0},{8,12},{12,8},{1,5},{5,1},{9,13},{13,9},{2,6},{6,2},{1... | collective-permute-start | bytes 3538952 | tf_op jit(solution)/shard_map/ppermute | solution.py:932
  240.1 29.0 %collective-permute-start.42 = (bf16[560,384]{1,0:T(8,128)(2,1)}, bf16[560,384]{1,0:T(8,128)(2,1)S(1)}, u32[]{:S(2)}, u32[]{:S(2)}) collective-permute-start(bf16[560,384]{1,0:T(8,128)(2,1)} %get-tuple-element.218), channel_id=1, source_target_pairs={{0,4},{4,0},{8,12},{12,8},{1,5},{5,1},{9,13},{13,9},{2,6},{6,2},{1... | collective-permute-start | bytes 1290248 | tf_op jit(solution)/shard_map/ppermute | solution.py:932
  240.5 28.5 %collective-permute-start.43 = (bf16[560,384]{1,0:T(8,128)(2,1)}, bf16[560,384]{1,0:T(8,128)(2,1)S(1)}, u32[]{:S(2)}, u32[]{:S(2)}) collective-permute-start(bf16[560,384]{1,0:T(8,128)(2,1)} %get-tuple-element.219), channel_id=1, source_target_pairs={{0,8},{4,12},{8,0},{12,4},{1,9},{5,13},{9,1},{13,5},{2,10},{6,14},... | collective-permute-start | bytes 1290248 | tf_op jit(solution)/shard_map/ppermute | solution.py:932
  241.7 27.4 %collective-permute-start.44 = (bf16[560,384]{1,0:T(8,128)(2,1)}, bf16[560,384]{1,0:T(8,128)(2,1)S(1)}, u32[]{:S(2)}, u32[]{:S(2)}) collective-permute-start(bf16[560,384]{1,0:T(8,128)(2,1)} %get-tuple-element.220), channel_id=1, source_target_pairs={{0,12},{4,8},{8,4},{12,0},{1,13},{5,9},{9,5},{13,1},{2,14},{6,10},... | collective-permute-start | bytes 1290248 | tf_op jit(solution)/shard_map/ppermute | solution.py:932
  271.7 24.6 %collective-permute-start.48 = (bf16[64,768]{1,0:T(8,128)(2,1)}, bf16[64,768]{1,0:T(8,128)(2,1)S(1)}, u32[]{:S(2)}, u32[]{:S(2)}) collective-permute-start(bf16[64,768]{1,0:T(8,128)(2,1)} %get-tuple-element.257), channel_id=1, source_target_pairs={{0,4},{4,0},{8,12},{12,8},{1,5},{5,1},{9,13},{13,9},{2,6},{6,2},{1... | collective-permute-start | bytes 294920 | tf_op jit(solution)/shard_map/ppermute | solution.py:932
  272.4 23.9 %collective-permute-start.49 = (bf16[64,768]{1,0:T(8,128)(2,1)}, bf16[64,768]{1,0:T(8,128)(2,1)S(1)}, u32[]{:S(2)}, u32[]{:S(2)}) collective-permute-start(bf16[64,768]{1,0:T(8,128)(2,1)} %get-tuple-element.258), channel_id=1, source_target_pairs={{0,8},{4,12},{8,0},{12,4},{1,9},{5,13},{9,1},{13,5},{2,10},{6,14},... | collective-permute-start | bytes 294920 | tf_op jit(solution)/shard_map/ppermute | solution.py:932
  273.6 22.8 %collective-permute-start.50 = (bf16[64,768]{1,0:T(8,128)(2,1)}, bf16[64,768]{1,0:T(8,128)(2,1)S(1)}, u32[]{:S(2)}, u32[]{:S(2)}) collective-permute-start(bf16[64,768]{1,0:T(8,128)(2,1)} %get-tuple-element.259), channel_id=1, source_target_pairs={{0,12},{4,8},{8,4},{12,0},{1,13},{5,9},{9,5},{13,1},{2,14},{6,10},... | collective-permute-start | bytes 294920 | tf_op jit(solution)/shard_map/ppermute | solution.py:932
  285.8 35.0 %collective-permute-start.45 = (bf16[288,384]{1,0:T(8,128)(2,1)}, bf16[288,384]{1,0:T(8,128)(2,1)S(1)}, u32[]{:S(2)}, u32[]{:S(2)}) collective-permute-start(bf16[288,384]{1,0:T(8,128)(2,1)} %get-tuple-element.253), channel_id=1, source_target_pairs={{0,4},{4,0},{8,12},{12,8},{1,5},{5,1},{9,13},{13,9},{2,6},{6,2},{1... | collective-permute-start | bytes 663560 | tf_op jit(solution)/shard_map/ppermute | solution.py:932
  286.6 41.8 %collective-permute-start.46 = (bf16[288,384]{1,0:T(8,128)(2,1)}, bf16[288,384]{1,0:T(8,128)(2,1)S(1)}, u32[]{:S(2)}, u32[]{:S(2)}) collective-permute-start(bf16[288,384]{1,0:T(8,128)(2,1)} %get-tuple-element.254), channel_id=1, source_target_pairs={{0,8},{4,12},{8,0},{12,4},{1,9},{5,13},{9,1},{13,5},{2,10},{6,14},... | collective-permute-start | bytes 663560 | tf_op jit(solution)/shard_map/ppermute | solution.py:932
  (89 other events, 871.2 us)
